TPU v7x, 512 devices: a whole 4x8x8 slice. The times are simulated.
512 devices in a mesh: gy: 16 (over y, core), gz: 32 (over x, z).
Axes of the slice: x: 4, y: 8, z: 8, core: 2. Of those that a mesh axis runs over, the one named last changes fastest.
Arguments:
- fields: float32 [3, 132, 256, 4096], P(None, None, 'gy', 'gz'), may hold values from -25 to 25
Outputs:
- enstrophy: float32 [128, 256, 4096], P(None, 'gy', 'gz')
- strain_rate: float32 [128, 256, 4096], P(None, 'gy', 'gz')
- factor: float32 [128, 128], replicated
All inputs are finite; a program needn't handle non-finite values.
Results may differ from a plain program's by a relative error of at most 0.0003.
Values sent between devices are 32-bit elements; how exact they have to be, the bound alone decides.
A program may use at most 64 MiB of HBM per device.

v0:
```python
import jax
import jax.numpy as jnp
from jax import lax
from jax.sharding import PartitionSpec as P


def with_halo(cells, sides, width):
    for axis, dim in sides:
        count = lax.axis_size(axis)
        head = lax.slice_in_dim(cells, 0, width, axis=dim)
        tail = lax.slice_in_dim(cells, cells.shape[dim] - width, cells.shape[dim], axis=dim)
        cells = jnp.concatenate(
            [
                lax.ppermute(tail, axis, [(i, (i + 1) % count) for i in range(count)]),
                cells,
                lax.ppermute(head, axis, [((i + 1) % count, i) for i in range(count)]),
            ],
            axis=dim,
        )
    return cells


def stencil(minus_two, minus_one, plus_one, plus_two):
    return (minus_two - 8.0 * minus_one + 8.0 * plus_one - plus_two) / 12.0


def invariants(along_x, along_y, along_z):
    gradient = (along_x, along_y, along_z)
    strain_rate = (
        gradient[0][0] * gradient[0][0]
        + gradient[1][1] * gradient[1][1]
        + gradient[2][2] * gradient[2][2]
    )
    enstrophy = jnp.zeros_like(strain_rate)
    for source_axis, target_axis in ((0, 1), (0, 2), (1, 2)):
        rotation = gradient[source_axis][target_axis] - gradient[target_axis][source_axis]
        shearing = gradient[source_axis][target_axis] + gradient[target_axis][source_axis]
        enstrophy = enstrophy + 0.5 * rotation * rotation
        strain_rate = strain_rate + 0.5 * shearing * shearing
    return (enstrophy, strain_rate)


def per_device(fields):
    planes = fields.shape[1] - 4
    rows_y = fields.shape[2]
    cols_z = fields.shape[3]
    padded = with_halo(fields, (("gy", 2), ("gz", 3)), 2)
    inner = padded[:, :, 2 : rows_y + 2, 2 : cols_z + 2]
    along_x = stencil(
        inner[:, 0:planes],
        inner[:, 1 : planes + 1],
        inner[:, 3 : planes + 3],
        inner[:, 4 : planes + 4],
    )
    middle = padded[:, 2 : planes + 2]
    along_y = stencil(
        middle[:, :, 0:rows_y, 2 : cols_z + 2],
        middle[:, :, 1 : rows_y + 1, 2 : cols_z + 2],
        middle[:, :, 3 : rows_y + 3, 2 : cols_z + 2],
        middle[:, :, 4 : rows_y + 4, 2 : cols_z + 2],
    )
    along_z = stencil(
        middle[:, :, 2 : rows_y + 2, 0:cols_z],
        middle[:, :, 2 : rows_y + 2, 1 : cols_z + 1],
        middle[:, :, 2 : rows_y + 2, 3 : cols_z + 3],
        middle[:, :, 2 : rows_y + 2, 4 : cols_z + 4],
    )
    enstrophy, strain_rate = invariants(along_x, along_y, along_z)
    cells = rows_y * cols_z
    stacked = jnp.concatenate(
        [
            fields[:, 2 : planes + 2].reshape(3, planes, cells),
            enstrophy.reshape(1, planes, cells),
            strain_rate.reshape(1, planes, cells),
        ],
        axis=0,
    )
    local_grams = jnp.einsum(
        "fxc,fyc->fxy",
        stacked,
        stacked,
        precision=lax.Precision.HIGHEST,
        preferred_element_type=jnp.float32,
    )
    total_cells = cells * lax.axis_size("gy") * lax.axis_size("gz")
    local_squares = jnp.sum(stacked * stacked, axis=(1, 2))
    squares = lax.psum(local_squares, ("gy", "gz"))
    denominators = 5.0 * total_cells * (squares / (planes * total_cells) + 1e-06)
    local_cross = jnp.sum(local_grams / denominators[:, None, None], axis=0)
    cross = lax.psum(local_cross, ("gy", "gz"))
    factor = jnp.linalg.cholesky(cross)
    return (enstrophy, strain_rate, factor)


def solution(mesh):
    return jax.shard_map(
        per_device,
        mesh=mesh,
        in_specs=(P(None, None, "gy", "gz"),),
        out_specs=(P(None, "gy", "gz"), P(None, "gy", "gz"), P()),
        check_vma=False,
    )
```

profile of v0, /device:TPU:1, one launch (start us, length us, event | category | flops | bytes accessed | tf_op | source)
XLA Modules:
  0.0 479.2 jit_solution(11371910007592712357)
XLA Ops:
  7.2 0.0 all-reduce.2.cloned.1.call-start
  7.2 2.9 fusion.31
  10.2 2.7 collective-permute-start
  12.8 4.2 collective-permute-start.1
  17.0 6.6 %copy.25 = f32[3,132,16,128]{1,3,2,0:T(8,128)} copy(f32[3,132,16,128]{3,2,1,0:T(8,128)} %param.1) | data formatting | bytes 6488064 | tf_op args[0]
  23.6 1.9 slice-done.2
  25.5 2.4 reshape.229
  27.9 0.0 collective-permute-done
  27.9 1.3 copy.29
  29.2 0.0 copy-start.1
  29.2 0.0 collective-permute-done.1
  29.2 1.6 copy.32
  30.8 0.0 copy-start.2
  30.8 0.0 slice-start
  30.8 1.5 pad_maximum_fusion.16
  32.4 2.1 collective-permute-start.2
  34.4 0.0 slice-start.1
  34.4 8.8 %collective-permute-start.3 = (f32[3,132,20,2]{1,3,2,0:T(2,128)S(1)}, f32[3,132,20,2]{1,3,2,0:T(2,128)S(1)}, u32[]{:S(2)}, u32[]{:S(2)}) collective-permute-start(f32[3,132,20,2]{1,3,2,0:T(2,128)S(1)} %get-tuple-element.23), channel_id=1, source_target_pairs={{1,0},{2,1},{3,2},{4,3},{5,4},{6,5},{7,6},{8,7},{9,8},{10,9},{11,1... | collective-permute-start | bytes 190088 | tf_op jit(solution)/shard_map/ppermute | solution.py:16
  43.3 22.2 %fusion.11 = (f32[3,128,16,128]{1,3,2,0:T(8,128)S(1)}, f32[3,128,16,128]{1,3,2,0:T(8,128)S(1)}) fusion(f32[3,132,16,128]{1,3,2,0:T(8,128)} %copy.25, f32[3,132,2,128]{1,3,2,0:T(8,128)} %copy-done.2, f32[3,132,2,128]{1,3,2,0:T(8,128)} %copy-done.1), kind=kLoop, calls=%fused_computation.24 | loop fusion | flops 12582912 | bytes 26738688 | tf_op jit(solution)/shard_map/div | solution.py:24
  65.4 0.0 collective-permute-done.2
  65.5 0.0 collective-permute-done.3
  65.5 4.9 %fusion.2 = f32[3,128,16,128]{1,3,2,0:T(8,128)S(1)} fusion(f32[3,132,20,2]{1,3,2,0:T(2,128)S(1)} %collective-permute-done.3, f32[3,132,2,128]{1,3,2,0:T(8,128)} %copy-done.2, f32[3,132,16,128]{1,3,2,0:T(8,128)S(1)} %bitcast.28, f32[3,132,2,128]{1,3,2,0:T(8,128)} %copy-done.1, f32[3,132,20,2]{1,3,2,0:T(2,128)S(1)} %collective-permute-done.2), kind=kLoop, calls=%fused_computation.5 | loop fusion | flops 14155776 | bytes 7327488 | tf_op jit(solution)/shard_map/div | solution.py:24
  70.4 4.2 fusion.18
  74.6 2.6 copy.47
  77.2 2.6 copy.48
  79.9 1.3 copy.49
  81.2 2.6 copy.50
  83.8 1.3 copy.51
  85.2 1.3 copy.52
  86.5 1.3 copy.53
  87.8 4.2 fusion.20
  92.0 0.0 copy-start.7
  92.0 0.0 copy-start.8
  92.0 0.9 copy-done.7
  93.0 0.3 copy-done.8
  93.3 0.6 multiply_reduce_fusion
  93.9 96.1 %psum.14 = f32[5]{0:T(128)S(1)} all-reduce(f32[5]{0:T(128)S(1)} %multiply_reduce_fusion), channel_id=1, replica_groups=mesh['gy'=16,'gz'=32] {'gy','gz'}, use_global_device_ids=true, to_apply=%region_1.0 | all-reduce | flops 5 | bytes 40 | tf_op jit(solution)/shard_map/psum | solution.py:87
  190.0 7.3 %fusion.27 = f32[128,128]{1,0:T(8,128)S(1)} fusion(f32[1,128,2048]{2,1,0:T(8,128)} %copy-done.8, f32[1,128,2048]{2,1,0:T(8,128)} %copy-done.7, f32[3,128,2048]{2,1,0:T(8,128)S(1)} %copy-done, f32[5]{0:T(128)S(1)} %add_multiply_fusion), kind=kOutput, calls=%fused_computation.63 | convolution fusion | flops 2016034816 | bytes 5308436 | tf_op jit(solution)/shard_map/fxc,fyc->fxy/dot_general | solution.py:78
  197.3 0.7 copy.43
  198.0 0.0 all-reduce.2.cloned.1.call-update
  198.1 2.6 copy.45
  200.7 2.6 copy.46
  203.3 253.6 %all-reduce.2.cloned.1.call-done = f32[128,128]{0,1:T(8,128)} async-done(((f32[128,128]{0,1:T(8,128)}), f32[128,128]{0,1:T(8,128)}) %all-reduce.2.cloned.1.call-update) | async-done | bytes 65552 | tf_op jit(solution)/shard_map/psum | solution.py:90
  456.9 0.9 copy.44
  457.8 0.9 fusion.28
  458.7 11.7 %cholesky.18 = f32[128,128]{1,0:T(8,128)S(1)} custom-call(f32[128,128]{1,0:T(8,128)S(1)} %fusion.28), custom_call_target="Cholesky" | custom-call | tf_op jit(solution)/shard_map/jit(cholesky)/cholesky | solution.py:91
  470.4 0.7 compare_reduce_fusion
  471.1 1.3 select_select_fusion
  (18 shorter events, 0.1 us)
Async XLA Ops:
  7.2 449.7 %all-reduce.2.cloned.1.call-start = ((), (), s32[]{:S(2)}) async-start(), calls=%async_computation | async-start | bytes 131072 | tf_op jit(solution)/shard_map/psum | solution.py:90
  10.2 17.7 %collective-permute-start = (f32[3,132,2,128]{3,2,1,0:T(2,128)}, f32[3,132,2,128]{3,2,1,0:T(2,128)}, u32[]{:S(2)}, u32[]{:S(2)}) collective-permute-start(f32[3,132,2,128]{3,2,1,0:T(2,128)} %get-tuple-element.26), channel_id=1, source_target_pairs={{0,32},{32,64},{64,96},{96,128},{128,160},{160,192},{192,224},{224... | collective-permute-start | bytes 1216520 | tf_op jit(solution)/shard_map/ppermute | solution.py:14
  12.8 16.4 %collective-permute-start.1 = (f32[3,132,2,128]{3,2,1,0:T(2,128)S(1)}, f32[3,132,2,128]{3,2,1,0:T(2,128)}, u32[]{:S(2)}, u32[]{:S(2)}) collective-permute-start(f32[3,132,2,128]{3,2,1,0:T(2,128)S(1)} %get-tuple-element.27), channel_id=1, source_target_pairs={{32,0},{64,32},{96,64},{128,96},{160,128},{192,160},{224,192},{256... | collective-permute-start | bytes 1216520 | tf_op jit(solution)/shard_map/ppermute | solution.py:16
  23.6 1.9 slice-start.2
  29.2 3.2 copy-start.1
  30.8 1.6 copy-start.2
  30.8 34.7 %slice-start = ((s8[6291456]{0:T(1024)(128)(4,1)}), s8[4194304]{0:T(1024)(128)(4,1)S(1)}, s32[]{:S(2)}) async-start(s8[6291456]{0:T(1024)(128)(4,1)} %bitcast.27), calls=%async_computation.1 | async-start | bytes 8388608
  32.4 33.1 %collective-permute-start.2 = (f32[3,132,20,2]{1,3,2,0:T(2,128)S(1)}, f32[3,132,20,2]{1,3,2,0:T(2,128)S(1)}, u32[]{:S(2)}, u32[]{:S(2)}) collective-permute-start(f32[3,132,20,2]{1,3,2,0:T(2,128)S(1)} %get-tuple-element.22), channel_id=1, source_target_pairs={{0,1},{1,2},{2,3},{3,4},{4,5},{5,6},{6,7},{7,8},{8,9},{9,10},{10,1... | collective-permute-start | bytes 190088 | tf_op jit(solution)/shard_map/ppermute | solution.py:14
  34.4 31.1 %slice-start.1 = ((s8[6291456]{0:T(1024)(128)(4,1)}), s8[2097152]{0:T(1024)(128)(4,1)S(1)}, s32[]{:S(2)}) async-start(s8[6291456]{0:T(1024)(128)(4,1)} %bitcast.27), calls=%async_computation.2 | async-start | bytes 4194304
  34.4 31.0 %collective-permute-start.3 = (f32[3,132,20,2]{1,3,2,0:T(2,128)S(1)}, f32[3,132,20,2]{1,3,2,0:T(2,128)S(1)}, u32[]{:S(2)}, u32[]{:S(2)}) collective-permute-start(f32[3,132,20,2]{1,3,2,0:T(2,128)S(1)} %get-tuple-element.23), channel_id=1, source_target_pairs={{1,0},{2,1},{3,2},{4,3},{5,4},{6,5},{7,6},{8,7},{9,8},{10,9},{11,1... | collective-permute-start | bytes 190088 | tf_op jit(solution)/shard_map/ppermute | solution.py:16
  74.6 5.2 %copy-start.6 = (f32[1,128,16,128]{1,3,2,0:T(8,128)S(1)}, f32[1,128,16,128]{1,3,2,0:T(8,128)}, u32[]{:S(2)}) copy-start(f32[1,128,16,128]{1,3,2,0:T(8,128)} %get-tuple-element.19) | copy-start | bytes 3145732
  77.2 6.6 %copy-start.5 = (f32[1,128,16,128]{1,3,2,0:T(8,128)S(1)}, f32[1,128,16,128]{1,3,2,0:T(8,128)}, u32[]{:S(2)}) copy-start(f32[1,128,16,128]{1,3,2,0:T(8,128)} %get-tuple-element.11) | copy-start | bytes 3145732
  79.9 5.3 %copy-start.4 = (f32[1,128,16,128]{1,3,2,0:T(8,128)S(1)}, f32[1,128,16,128]{1,3,2,0:T(8,128)}, u32[]{:S(2)}) copy-start(f32[1,128,16,128]{1,3,2,0:T(8,128)} %get-tuple-element.12) | copy-start | bytes 3145732
  81.2 5.3 %copy-start.3 = (f32[1,128,16,128]{1,3,2,0:T(8,128)S(1)}, f32[1,128,16,128]{1,3,2,0:T(8,128)}, u32[]{:S(2)}) copy-start(f32[1,128,16,128]{1,3,2,0:T(8,128)} %get-tuple-element.13) | copy-start | bytes 3145732
  87.8 5.5 %copy-start = (f32[3,128,2048]{2,1,0:T(8,128)S(1)}, f32[3,128,2048]{2,1,0:T(8,128)}, u32[]{:S(2)}) copy-start(f32[3,128,2048]{2,1,0:T(8,128)} %reshape.229) | copy-start | bytes 9437188
  92.0 1.0 copy-start.7
  92.0 1.3 copy-start.8
Sparse Core Ops, SparseCore 0:
  198.2 258.6 all-reduce.1
where the time goes:
time: 480 us; the launch traced here: 479 us
  waiting for transfers between devices  254 us (53%)
  blocking collectives  96.1 us (20%)
  other arithmetic  52.2 us (11%)
  local copies, waits for them, and re-layouts  38 us (8%)
  starting transfers between devices  17.8 us (4%)
  between operations  14.2 us (3%)
  matrix products  7.3 us (2%)
    psum x1, waiting for transfers between devices, per_device(): cross = lax.psum(local_cross, ('gy', 'gz'))  254 us
    psum x1, blocking collectives, per_device(): squares = lax.psum(local_squares, ('gy', 'gz'))  96.1 us
    div x2, other arithmetic, stencil(): return (minus_two - 8.0 * minus_one + 8.0 * plus_one - plus_two) / 12.0  27.1 us
    unnamed x25, local copies, waits for them, and re-layouts  13.2 us
    ppermute x2, starting transfers between devices, with_halo(): lax.ppermute(head, axis, [((i + 1) % count, i) for i in range(count)])  13 us
    another operation x3, other arithmetic, per_device(): factor = jnp.linalg.cholesky(cross)  12.4 us
  transfers between devices with their start and end apart: 5, of which 1 were waited for; matrix products, arithmetic and copies ran while one was open for 8% of the time, Pallas kernels for 0%

commit v1 on v0

v1 whole, which is shorter than its diff:
```python
import jax
import jax.numpy as jnp
from jax import lax
from jax.experimental import pallas as pl
from jax.experimental.pallas import tpu as pltpu
from jax.sharding import PartitionSpec as P

MESH = pl.DeviceIdType.MESH
CORES = 2
N = 128
RY = 16
RZ = 128
X0 = 6
XC = X0 + 2
XB = 16
F32 = jnp.float32
BF16 = jnp.bfloat16


def ring_order(count):
    return sorted(range(1, count), key=lambda k: -min(k, count - k))


def main_kernel(
    sizes,
    fields,
    enst,
    strn,
    cross_out,
    fld,
    pack_r,
    pack_l,
    from_left,
    from_right,
    merged,
    dxw_buf,
    dyw_buf,
    halves,
    piece,
    recv_a,
    sum_a,
    recv_b,
    sum_b,
    recv_c,
    comb,
    load_sem,
    halo_send,
    halo_recv,
    rs_send,
    rs_recv,
    ey_send,
    ey_recv,
    ez_send,
    ez_recv,
    ag_send,
    ag_recv,
):
    gy, gz, zc = sizes
    yc, xc = gy // CORES, gz // zc
    owners = xc * CORES
    own_rows = N // owners
    cells = gy * RY * gz * RZ
    g, h = lax.axis_index("gy"), lax.axis_index("gz")
    y, c = g // CORES, g % CORES
    x, z = h // zc, h % zc

    rs_peers = []
    for dx in ring_order(xc) + [0]:
        for dc in range(CORES):
            if dx or dc:
                slot = dx * CORES + dc - 1
                px, pc = lax.rem(x + dx, xc), lax.rem(c + dc, CORES)
                rs_peers.append((slot, px * CORES + pc, (y * CORES + pc, px * zc + z)))
    ey_peers = [(k - 1, (lax.rem(y + k, yc) * CORES + c, h)) for k in ring_order(yc)]
    ez_peers = [(k - 1, (g, x * zc + lax.rem(z + k, zc))) for k in ring_order(zc)]
    me = x * CORES + c
    up, down = (lax.rem(g + 1, gy), h), (lax.rem(g + gy - 1, gy), h)
    right, left = (g, lax.rem(h + 1, gz)), (g, lax.rem(h + gz - 1, gz))

    barrier = pltpu.get_barrier_semaphore()
    peers = [p for _, p in ey_peers + ez_peers] + [p for _, _, p in rs_peers] + [up, down, right, left]
    for p in peers:
        pl.semaphore_signal(barrier, inc=1, device_id=p, device_id_type=MESH)

    def load(f, row):
        return pltpu.make_async_copy(
            fields.at[f, :, row, :], fld.at[f, row + 2, pl.ds(X0, N + 4), :], load_sem.at[0 if row in faces else 1]
        )

    faces = (0, 1, RY - 2, RY - 1)
    face_loads = [load(f, r) for r in faces for f in range(3)]
    rest_loads = [load(f, r) for r in range(RY) if r not in faces for f in range(3)]
    for cp in face_loads + rest_loads:
        cp.start()
    for cp in face_loads:
        cp.wait()
    pl.semaphore_wait(barrier, len(peers))

    sends = []
    window = pl.ds(XC, N)
    for f in range(3):
        for r in range(2):
            for way, (src, dst, to) in enumerate(((RY + r, r, up), (2 + r, RY + 2 + r, down))):
                slot = way * 6 + f * 2 + r
                sends.append(
                    pltpu.make_async_remote_copy(
                        src_ref=fld.at[f, src, window, :],
                        dst_ref=fld.at[f, dst, window, :],
                        send_sem=halo_send.at[slot],
                        recv_sem=halo_recv.at[slot],
                        device_id=to,
                        device_id_type=MESH,
                    )
                )
    y_halo = list(sends)
    for cp in y_halo:
        cp.start()
    for cp in rest_loads:
        cp.wait()

    lane = lax.broadcasted_iota(jnp.int32, (XB, RZ), 1)
    group = lane // 4
    low_half = lane % 4 < 2

    def pack(b, carry):
        row = pl.multiple_of(XC + b * XB, 8)
        packs = [jnp.zeros((XB, RZ), F32) for _ in range(2)]
        for t in range(3 * RY):
            j = t % 32
            v = fld[t // RY, t % RY + 2, pl.ds(row, XB), :]
            v = pltpu.roll(v, (4 * j + 2) % RZ, 1)
            packs[t // 32] = jnp.where(group == j, v, packs[t // 32])
        out = pl.ds(pl.multiple_of(b * XB, XB), XB)
        pack_r[out, :] = jnp.where(low_half, packs[0], pltpu.roll(packs[1], 2, 1))
        pack_l[out, :] = jnp.where(low_half, pltpu.roll(packs[0], RZ - 2, 1), packs[1])
        return carry

    lax.fori_loop(0, N // XB, pack, 0)
    z_halo = [
        pltpu.make_async_remote_copy(
            src_ref=src,
            dst_ref=dst,
            send_sem=halo_send.at[12 + i],
            recv_sem=halo_recv.at[12 + i],
            device_id=to,
            device_id_type=MESH,
        )
        for i, (src, dst, to) in enumerate(((pack_r, from_left, right), (pack_l, from_right, left)))
    ]
    for cp in z_halo:
        cp.start()
    sends += z_halo

    def split_store(q, row, b, value):
        high = value.astype(BF16)
        cols = pl.ds(pl.multiple_of(row * RZ, RZ), RZ)
        halves[q, pl.ds(b * XB, XB), cols] = high
        halves[q, pl.ds(N + b * XB, XB), cols] = (value - high.astype(F32)).astype(BF16)

    def split_fields(row, carry):
        for f in range(3):
            for b in range(N // XB):
                split_store(f, row, b, fld[f, row + 2, pl.ds(XC + b * XB, XB), :])
        return carry

    lax.fori_loop(0, RY, split_fields, 0)

    eye = lax.broadcasted_iota(jnp.int32, (N, N), 0) == lax.broadcasted_iota(jnp.int32, (N, N), 1)
    below = lax.broadcasted_iota(jnp.int32, (N, N), 0) > lax.broadcasted_iota(jnp.int32, (N, N), 1)

    def gram(q):
        both = halves[q]
        full = lax.dot_general(both, both, (((1,), (1,)), ((), ())), preferred_element_type=F32)
        return full[:N, :N] + full[:N, N:] + full[N:, :N] + full[N:, N:]

    def diagonal(m):
        return jnp.sum(jnp.where(eye, m, 0.0), axis=0, keepdims=True)

    def scatter_store(square, value):
        for o in range(owners):
            piece[o, square * own_rows:(square + 1) * own_rows, :] = value[o * own_rows:(o + 1) * own_rows, :]

    gu, gv, gw = gram(0), gram(1), gram(2)
    scatter_store(0, jnp.where(below, gu, gv))
    diags = [diagonal(m) for m in (gu, gv, gw)]

    def derivative(m2, m1, p1, p2):
        return 8.0 * (p1 - m1) + (m2 - p2)

    def without_z(row, carry):
        for b in range(N // XB):
            at = XC + b * XB

            def dx(f):
                return derivative(*(fld[f, row + 2, pl.ds(at + k, XB), :] for k in (-2, -1, 1, 2)))

            def dy(f):
                return derivative(*(fld[f, row + 2 + k, pl.ds(at, XB), :] for k in (-2, -1, 1, 2)))

            here = pl.ds(b * XB, XB)
            dxu, dxv, dyu, dyv = dx(0), dx(1), dy(0), dy(1)
            rotation, shear = dxv - dyu, dxv + dyu
            enst[row, here, :] = rotation * rotation
            strn[row, here, :] = 2.0 * (dxu * dxu + dyv * dyv) + shear * shear
            dxw_buf[row, here, :] = dx(2)
            dyw_buf[row, here, :] = dy(2)
        return carry

    def with_z(row, carry):
        for b in range(N // XB):
            here = pl.ds(b * XB, XB)

            def dz(f):
                tile = f * RY + row
                shift = lax.rem(RZ + RZ - 2 - 4 * lax.rem(tile, 32), RZ)
                edge = pltpu.roll(merged[0 if f < 2 else 1, here, :], shift, 1)
                v = fld[f, row + 2, pl.ds(XC + b * XB, XB), :]
                m1 = pltpu.roll(jnp.where(lane == RZ - 1, edge, v), 1, 1)
                m2 = pltpu.roll(jnp.where(lane >= RZ - 2, edge, v), 2, 1)
                p1 = pltpu.roll(jnp.where(lane == 0, edge, v), RZ - 1, 1)
                p2 = pltpu.roll(jnp.where(lane < 2, edge, v), RZ - 2, 1)
                return derivative(m2, m1, p1, p2)

            dzu, dzv, dzw = dz(0), dz(1), dz(2)
            dxw, dyw = dxw_buf[row, here, :], dyw_buf[row, here, :]
            r1, r2, s1, s2 = dxw - dzu, dyw - dzv, dxw + dzu, dyw + dzv
            e = (enst[row, here, :] + r1 * r1 + r2 * r2) * (1.0 / 288.0)
            s = (strn[row, here, :] + 2.0 * dzw * dzw + s1 * s1 + s2 * s2) * (1.0 / 288.0)
            enst[row, here, :] = e
            strn[row, here, :] = s
            split_store(3, row, b, e)
            split_store(4, row, b, s)
        return carry

    lax.fori_loop(2, RY - 2, without_z, 0)
    for cp in z_halo:
        cp.wait_recv()

    def merge(b, carry):
        here = pl.ds(pl.multiple_of(b * XB, XB), XB)
        lo, hi = from_left[here, :], from_right[here, :]
        merged[0, here, :] = jnp.where(low_half, lo, pltpu.roll(hi, 2, 1))
        merged[1, here, :] = jnp.where(low_half, pltpu.roll(lo, RZ - 2, 1), hi)
        return carry

    lax.fori_loop(0, N // XB, merge, 0)
    lax.fori_loop(2, RY - 2, with_z, 0)
    for cp in y_halo:
        cp.wait_recv()

    def face_row(i, carry):
        row = i + (RY - 4) * (i // 2)
        without_z(row, 0)
        with_z(row, 0)
        return carry

    lax.fori_loop(0, 4, face_row, 0)
    ge, gs = gram(3), gram(4)
    scatter_store(1, jnp.where(below, gw, gs))
    scatter_store(2, jnp.where(below, ge, 0.0))
    diags += [diagonal(ge), diagonal(gs), jnp.zeros((3, N), F32)]
    tail = jnp.concatenate(diags, axis=0)
    for o in range(owners):
        piece[o, 3 * own_rows:, :] = tail

    def exchange(copies, recv, own):
        for cp in copies:
            cp.start()
        for cp in copies:
            cp.wait_recv()
        total = own
        for k in range(recv.shape[0]):
            total = total + recv[k]
        return total

    rs = [
        pltpu.make_async_remote_copy(
            src_ref=piece.at[o],
            dst_ref=recv_a.at[slot],
            send_sem=rs_send.at[slot],
            recv_sem=rs_recv.at[slot],
            device_id=to,
            device_id_type=MESH,
        )
        for slot, o, to in rs_peers
    ]
    sum_a[...] = exchange(rs, recv_a, piece[me])
    ey = [
        pltpu.make_async_remote_copy(
            src_ref=sum_a,
            dst_ref=recv_b.at[slot],
            send_sem=ey_send.at[slot],
            recv_sem=ey_recv.at[slot],
            device_id=to,
            device_id_type=MESH,
        )
        for slot, to in ey_peers
    ]
    sum_b[...] = exchange(ey, recv_b, sum_a[...])
    ez = [
        pltpu.make_async_remote_copy(
            src_ref=sum_b,
            dst_ref=recv_c.at[slot],
            send_sem=ez_send.at[slot],
            recv_sem=ez_recv.at[slot],
            device_id=to,
            device_id_type=MESH,
        )
        for slot, to in ez_peers
    ]
    total = exchange(ez, recv_c, sum_b[...])

    diag = total[3 * own_rows:, :]
    trace = jnp.sum(diag, axis=1, keepdims=True)
    weight = 1.0 / (5.0 * cells * (trace / (N * cells) + 1e-6))
    weights = [jnp.broadcast_to(weight[q:q + 1, :], (own_rows, N)) for q in range(5)]
    row_id = me * own_rows + lax.broadcasted_iota(jnp.int32, (own_rows, N), 0)
    lower = row_id > lax.broadcasted_iota(jnp.int32, (own_rows, N), 1)
    s0, s1, s2 = (total[q * own_rows:(q + 1) * own_rows, :] for q in range(3))
    w0 = jnp.where(lower, weights[0], weights[1])
    w1 = jnp.where(lower, weights[2], weights[4])
    mine = pl.ds(pl.multiple_of(me * own_rows, own_rows), own_rows)
    comb[mine, :] = s0 * w0 + s1 * w1 + s2 * weights[3]
    ag = [
        pltpu.make_async_remote_copy(
            src_ref=comb.at[mine, :],
            dst_ref=comb.at[mine, :],
            send_sem=ag_send.at[slot],
            recv_sem=ag_recv.at[slot],
            device_id=to,
            device_id_type=MESH,
        )
        for slot, _, to in rs_peers
    ]
    for cp in ag:
        cp.start()
    for cp in sends + rs + ey + ez:
        cp.wait_send()
    five = lax.broadcasted_iota(jnp.int32, diag.shape, 0) < 5
    middle = jnp.sum(jnp.where(five, diag * weight, 0.0), axis=0, keepdims=True)
    for cp in ag:
        cp.wait_recv()
    square = comb[...]
    half = jnp.where(below, square, 0.0) + jnp.where(below, square.T, 0.0)
    cross_out[...] = half + half.T + jnp.where(eye, jnp.broadcast_to(middle, (N, N)), 0.0)
    for cp in ag:
        cp.wait_send()


def split3(v):
    high = v.astype(BF16).astype(F32)
    rest = v - high
    middle = rest.astype(BF16).astype(F32)
    return high, middle, rest - middle


def factor_kernel(cross, e_in, s_in, e_out, s_out, factor, work, upper, out_sem):
    stores = [
        pltpu.make_async_copy(src.at[r], dst.at[:, r, :], out_sem.at[q, r])
        for q, (src, dst) in enumerate(((e_in, e_out), (s_in, s_out)))
        for r in range(RY)
    ]
    for cp in stores:
        cp.start()
    work[...] = cross[...]
    lane = lax.broadcasted_iota(jnp.int32, (8, N), 1)
    sub = lax.broadcasted_iota(jnp.int32, (8, N), 0)
    for p in range(N // 8):
        base = 8 * p
        v = work[base:base + 8, :]
        rows = [jnp.broadcast_to(v[k:k + 1, :], (8, N)) for k in range(8)]
        s = {}
        for k in range(8):
            for m in range(k, 8):
                s[k, m] = jnp.broadcast_to(rows[k][:, base + m:base + m + 1], (8, N))
        panel = None
        for k in range(8):
            r = lax.rsqrt(s[k, k])
            u = {m: s[k, m] * r for m in range(k + 1, 8)}
            for m in range(k + 1, 8):
                for q in range(m, 8):
                    s[m, q] = s[m, q] - u[m] * u[q]
            rows[k] = rows[k] * r
            for m in range(k + 1, 8):
                rows[m] = rows[m] - u[m] * rows[k]
            panel = rows[k] if panel is None else jnp.where(sub == k, rows[k], panel)
        upper[base:base + 8, :] = jnp.where(lane >= sub + base, panel, 0.0)
        if p < N // 8 - 1:
            hi, mid, lo = split3(panel)
            lhs = jnp.concatenate([hi, hi, mid, mid, hi, lo], axis=0).astype(BF16)
            rhs = jnp.concatenate([hi, mid, hi, mid, lo, hi], axis=0).astype(BF16)
            update = lax.dot_general(lhs, rhs, (((0,), (0,)), ((), ())), preferred_element_type=F32)
            work[base + 8:, :] = work[base + 8:, :] - update[base + 8:, :]
    factor[...] = upper[...].T
    for cp in stores:
        cp.wait()


def per_device(sizes, fields):
    gy, gz, zc = sizes
    yc, xc = gy // CORES, gz // zc
    owners = xc * CORES
    rows = 3 * (N // owners) + 8
    vmem = pl.BlockSpec(memory_space=pltpu.VMEM)
    anywhere = pl.BlockSpec(memory_space=pl.ANY)
    hbm = pl.BlockSpec(memory_space=pltpu.HBM)
    grid_rows = jax.ShapeDtypeStruct((RY, N, RZ), F32)
    dma = pltpu.SemaphoreType.DMA

    def body(*refs):
        main_kernel(sizes, *refs)

    e, s, cross = pl.pallas_call(
        body,
        out_shape=(grid_rows, grid_rows, jax.ShapeDtypeStruct((N, N), F32)),
        in_specs=[hbm],
        out_specs=(vmem, vmem, vmem),
        scratch_shapes=[
            pltpu.VMEM((3, RY + 4, N + 16, RZ), F32),
            pltpu.VMEM((N, RZ), F32),
            pltpu.VMEM((N, RZ), F32),
            pltpu.VMEM((N, RZ), F32),
            pltpu.VMEM((N, RZ), F32),
            pltpu.VMEM((2, N, RZ), F32),
            pltpu.VMEM((RY, N, RZ), F32),
            pltpu.VMEM((RY, N, RZ), F32),
            pltpu.VMEM((5, 2 * N, RY * RZ), BF16),
            pltpu.VMEM((owners, rows, N), F32),
            pltpu.VMEM((owners - 1, rows, N), F32),
            pltpu.VMEM((rows, N), F32),
            pltpu.VMEM((yc - 1, rows, N), F32),
            pltpu.VMEM((rows, N), F32),
            pltpu.VMEM((zc - 1, rows, N), F32),
            pltpu.VMEM((N, N), F32),
            dma((2,)),
            dma((14,)),
            dma((14,)),
            dma((owners - 1,)),
            dma((owners - 1,)),
            dma((yc - 1,)),
            dma((yc - 1,)),
            dma((zc - 1,)),
            dma((zc - 1,)),
            dma((owners - 1,)),
            dma((owners - 1,)),
        ],
        compiler_params=pltpu.CompilerParams(collective_id=0, has_side_effects=True, vmem_limit_bytes=48 << 20),
        name="stencil_gram",
    )(pltpu.with_memory_space_constraint(fields, pltpu.HBM))
    whole = jax.ShapeDtypeStruct((N, RY, RZ), F32)
    return pl.pallas_call(
        factor_kernel,
        out_shape=(whole, whole, jax.ShapeDtypeStruct((N, N), F32)),
        in_specs=[vmem, vmem, vmem],
        out_specs=(anywhere, anywhere, vmem),
        scratch_shapes=[
            pltpu.VMEM((N, N), F32),
            pltpu.VMEM((N, N), F32),
            dma((2, RY)),
        ],
        compiler_params=pltpu.CompilerParams(vmem_limit_bytes=16 << 20),
        name="factor",
    )(cross, e, s)


def solution(mesh):
    gy, gz = mesh.shape["gy"], mesh.shape["gz"]
    sizes = (gy, gz, 8 if gz % 8 == 0 else 2)

    def call(fields):
        return per_device(sizes, fields)

    return jax.shard_map(
        call,
        mesh=mesh,
        in_specs=(P(None, None, "gy", "gz"),),
        out_specs=(P(None, "gy", "gz"), P(None, "gy", "gz"), P()),
        check_vma=False,
    )
```

time: 480 us -> 69.2 us (0.14)
  waiting for transfers between devices: 254 us -> 0 us
  blocking collectives: 96.1 us -> 0 us
  Pallas kernels: 0 us -> 68.4 us
  other arithmetic: 52.2 us -> 0 us
  local copies, waits for them, and re-layouts: 38 us -> 0 us
  starting transfers between devices: 17.8 us -> 0 us
  between operations: 14.2 us -> 0.64 us
  matrix products: 7.3 us -> 0 us
    psum x1 -> x0, waiting for transfers between devices: 254 us -> none  [per_device(): cross = lax.psum(local_cross, ('gy', 'gz'))]
    psum x1 -> x0, blocking collectives: 96.1 us -> none  [per_device(): squares = lax.psum(local_squares, ('gy', 'gz'))]
    pallas_call x0 -> x2, Pallas kernels: none -> 68.4 us  [the longest x1 60.5 us: per_device(): pl.pallas_call(body, out_shape=(grid_rows, grid_rows, jax.ShapeDtypeStruc...]
    div x3 -> x0, other arithmetic: 27.9 us -> none  [the longest x2 27.1 us: stencil(): return (minus_two - 8.0 * minus_one + 8.0 * plus_one - plus_two) / 12.0]
    ppermute x4 -> x0, starting transfers between devices: 17.7 us -> none  [the longest x2 13 us: with_halo(): lax.ppermute(head, axis, [((i + 1) % count, i) for i in range(count)])]
    unnamed x25 -> x0, local copies, waits for them, and re-layouts: 13.2 us -> none
    another operation x3 -> x0, other arithmetic: 12.4 us -> none  [per_device(): factor = jnp.linalg.cholesky(cross)]
    add x2 -> x0, other arithmetic: 8.42 us -> none  [the longest x1 4.21 us: invariants(): enstrophy = enstrophy + 0.5 * rotation * rotation]
  transfers between devices with their start and end apart: 5 -> 0, of which waited for: 1 -> 0; matrix products, arithmetic and copies ran while one was open for 8% -> 0% of each run, Pallas kernels for 0% -> 0%
where the time goes in v1:
time: 69.2 us; the launch traced here: 69 us
  Pallas kernels  68.4 us (99%)
    pallas_call x1, Pallas kernels, per_device(): pl.pallas_call(body, out_shape=(grid_rows, grid_rows, jax.ShapeDtypeStruc...  60.5 us
    pallas_call x1, Pallas kernels, per_device(): pl.pallas_call(factor_kernel, out_shape=(whole, whole, jax.ShapeDtypeStru...  7.91 us

profile of v1, /device:TPU:1, one launch (start us, length us, event | category | flops | bytes accessed | tf_op | source)
XLA Modules:
  0.0 69.0 jit_solution(5715665940637595831)
XLA Ops:
  0.6 60.5 %stencil_gram.1 = (f32[16,128,128]{2,1,0:T(8,128)S(1)}, f32[16,128,128]{2,1,0:T(8,128)S(1)}, f32[128,128]{1,0:T(8,128)S(1)}) custom-call(f32[3,132,16,128]{3,2,1,0:T(8,128)} %refs_0_.1), custom_call_target="tpu_custom_call" | custom-call | tf_op jit(solution)/shard_map/stencil_gram/pallas_call | solution.py:413
  61.1 7.9 %factor.1 = (f32[128,16,128]{2,1,0:T(8,128)}, f32[128,16,128]{2,1,0:T(8,128)}, f32[128,128]{1,0:T(8,128)}) custom-call(f32[128,128]{1,0:T(8,128)S(1)} %get-tuple-element.6.cross, f32[16,128,128]{2,1,0:T(8,128)S(1)} %get-tuple-element.7.e_in, f32[16,128,128]{2,1,0:T(8,128)S(1)} %get-tuple-element.8.s_in), custom_call_target="tpu_custom_call" | custom-call | tf_op jit(solution)/shard_map/factor/pallas_call | solution.py:451

commit v2 on v1

v2 whole, which is shorter than its diff:
```python
import jax
import jax.numpy as jnp
from jax import lax
from jax.experimental import pallas as pl
from jax.experimental.pallas import tpu as pltpu
from jax.sharding import PartitionSpec as P

MESH = pl.DeviceIdType.MESH
CORES = 2
N = 128
RY = 16
RZ = 128
X0 = 6
XC = X0 + 2
XB = 16
F32 = jnp.float32
BF16 = jnp.bfloat16


def ring_order(count):
    return sorted(range(1, count), key=lambda k: -min(k, count - k))


def main_kernel(
    sizes,
    fields,
    enst,
    strn,
    cross_out,
    fld,
    pack_r,
    pack_l,
    from_left,
    from_right,
    edges,
    dz_buf,
    dxw_buf,
    dyw_buf,
    halves,
    thirds,
    band,
    grams,
    comb,
    load_sem,
    halo_send,
    halo_recv,
    ag_send,
    ag_recv,
    *channels,
):
    gy, gz, zc = sizes
    yc, xc = gy // CORES, gz // zc
    owners = xc * CORES
    own_rows = N // owners
    cells = gy * RY * gz * RZ
    g, h = lax.axis_index("gy"), lax.axis_index("gz")
    y, c = g // CORES, lax.rem(g, CORES)
    x, z = h // zc, lax.rem(h, zc)

    rs_peers = []
    for dx in ring_order(xc) + [0]:
        for dc in range(CORES):
            if dx or dc:
                slot = dx * CORES + dc - 1
                px, pc = lax.rem(x + dx, xc), lax.rem(c + dc, CORES)
                rs_peers.append((slot, px * CORES + pc, (y * CORES + pc, px * zc + z)))
    ey_peers = [(k - 1, (lax.rem(y + k, yc) * CORES + c, h)) for k in ring_order(yc)]
    ez_peers = [(k - 1, (g, x * zc + lax.rem(z + k, zc))) for k in ring_order(zc)]
    me = x * CORES + c
    up, down = (lax.rem(g + 1, gy), h), (lax.rem(g + gy - 1, gy), h)
    right, left = (g, lax.rem(h + 1, gz)), (g, lax.rem(h + gz - 1, gz))

    def remote(src, dst, send, recv, to):
        return pltpu.make_async_remote_copy(
            src_ref=src, dst_ref=dst, send_sem=send, recv_sem=recv, device_id=to, device_id_type=MESH
        )

    def load(row):
        return pltpu.make_async_copy(fields.at[:, :, row, :], fld.at[:, row + 2, pl.ds(X0, N + 4), :], load_sem.at[row])

    faces = (0, 1, RY - 2, RY - 1)
    for row in faces + tuple(range(2, RY - 2)):
        load(row).start()

    barrier = pltpu.get_barrier_semaphore()
    peers = [p for _, p in ey_peers + ez_peers] + [p for _, _, p in rs_peers] + [up, down, right, left]
    for p in peers:
        pl.semaphore_signal(barrier, inc=1, device_id=p, device_id_type=MESH)
    for row in faces:
        load(row).wait()
    pl.semaphore_wait(barrier, len(peers))

    window = pl.ds(XC, N)

    def y_copy(way, r):
        slot = way * 2 + r
        src, dst = 2 + r + (RY - 2) * (1 - way), r + (RY + 2) * way
        to = (lax.rem(g + 1 + (gy - 2) * way, gy), h)
        return remote(
            fld.at[:, src, window, :], fld.at[:, dst, window, :], halo_send.at[slot], halo_recv.at[slot], to
        )

    sends = [y_copy(way, r) for way in range(2) for r in range(2)]
    for cp in sends:
        cp.start()

    def three_way(value):
        high = value.astype(BF16)
        rest = value - high.astype(F32)
        middle = rest.astype(BF16)
        return high, middle, (rest - middle.astype(F32)).astype(BF16)

    def split_fields(row):
        cols = pl.ds(pl.multiple_of(row * RZ, RZ), RZ)
        for f in range(3):
            for b in range(N // XB):
                high, middle, low = three_way(fld[f, row + 2, pl.ds(XC + b * XB, XB), :])
                halves[f, pl.ds(b * XB, XB), cols] = high
                halves[f, pl.ds(N + b * XB, XB), cols] = middle
                thirds[f, pl.ds(b * XB, XB), cols] = low

    def split_face(i, carry):
        split_fields(i + (RY - 4) * (i // 2))
        return carry

    def split_rest(row, carry):
        load(row).wait()
        split_fields(row)
        return carry

    lax.fori_loop(0, 4, split_face, 0)
    lax.fori_loop(2, RY - 2, split_rest, 0)

    lane = lax.broadcasted_iota(jnp.int32, (XB, RZ), 1)
    group = lane // 4
    member = lane % 4
    low_half = member < 2

    def pack(b, carry):
        row = pl.multiple_of(XC + b * XB, 8)
        packs = [jnp.zeros((XB, RZ), F32) for _ in range(2)]
        for t in range(3 * RY):
            j = t % 32
            v = fld[t // RY, t % RY + 2, pl.ds(row, XB), :]
            v = pltpu.roll(v, (4 * j + 2) % RZ, 1)
            packs[t // 32] = jnp.where(group == j, v, packs[t // 32])
        out = pl.ds(pl.multiple_of(b * XB, XB), XB)
        pack_r[out, :] = jnp.where(low_half, packs[0], pltpu.roll(packs[1], 2, 1))
        pack_l[out, :] = jnp.where(low_half, pltpu.roll(packs[0], RZ - 2, 1), packs[1])
        return carry

    lax.fori_loop(0, N // XB, pack, 0)
    z_halo = [
        remote(pack_r, from_left, halo_send.at[4], halo_recv.at[4], right),
        remote(pack_l, from_right, halo_send.at[5], halo_recv.at[5], left),
    ]
    for cp in z_halo:
        cp.start()
    sends += z_halo

    eye = lax.broadcasted_iota(jnp.int32, (N, N), 0) == lax.broadcasted_iota(jnp.int32, (N, N), 1)
    below = lax.broadcasted_iota(jnp.int32, (N, N), 0) > lax.broadcasted_iota(jnp.int32, (N, N), 1)

    def gram(q, cols):
        both = halves[q, :, cols]
        full = lax.dot_general(both, both, (((1,), (1,)), ((), ())), preferred_element_type=F32)
        return full[:N, :N] + full[:N, N:] + full[N:, :N] + full[N:, N:]

    def diagonal(m):
        return jnp.sum(jnp.where(eye, m, 0.0), axis=0, keepdims=True)

    def fill(piece, squares, diags):
        tail = jnp.concatenate(diags + [jnp.zeros((8 - len(diags), N), F32)], axis=0)
        for o in range(owners):
            for k, value in enumerate(squares):
                piece[o, k * own_rows:(k + 1) * own_rows, :] = value[o * own_rows:(o + 1) * own_rows, :]
            piece[o, len(squares) * own_rows:, :] = tail

    class Channel:
        def __init__(self, piece, recv_a, sum_a, recv_b, sum_b, recv_c, rs_s, rs_r, ey_s, ey_r, ez_s, ez_r):
            self.piece, self.recv_a, self.sum_a = piece, recv_a, sum_a
            self.recv_b, self.sum_b, self.recv_c = recv_b, sum_b, recv_c
            self.rs = [remote(piece.at[o], recv_a.at[k], rs_s.at[k], rs_r.at[k], to) for k, o, to in rs_peers]
            self.ey = [remote(sum_a, recv_b.at[k], ey_s.at[k], ey_r.at[k], to) for k, to in ey_peers]
            self.ez = [remote(sum_b, recv_c.at[k], ez_s.at[k], ez_r.at[k], to) for k, to in ez_peers]

        def start(self, copies):
            for cp in copies:
                cp.start()

        def collect(self, copies, recv, own):
            for cp in copies:
                cp.wait_recv()
            for k in range(recv.shape[0]):
                own = own + recv[k]
            return own

        def scatter(self):
            self.start(self.rs)

        def along_y(self):
            self.sum_a[...] = self.collect(self.rs, self.recv_a, self.piece[me])
            self.start(self.ey)

        def along_z(self):
            self.sum_b[...] = self.collect(self.ey, self.recv_b, self.sum_a[...])
            self.start(self.ez)

        def total(self):
            return self.collect(self.ez, self.recv_c, self.sum_b[...])

    early, late = Channel(*channels[:12]), Channel(*channels[12:])
    everything = pl.ds(0, RY * RZ)
    gu, gv, gw = (gram(f, everything) for f in range(3))
    fill(early.piece, [jnp.where(below, gu, gv), gw], [diagonal(m) for m in (gu, gv, gw)])
    early.scatter()

    wide = 2 * RZ
    depth = lax.broadcasted_iota(jnp.int32, (3 * wide, wide), 0) % wide
    column = lax.broadcasted_iota(jnp.int32, (3 * wide, wide), 1)
    step = jnp.where(depth // RZ == column // RZ, column - depth, 0)
    weights = jnp.where(step == 2, 1.0, 0.0) - jnp.where(step == -2, 1.0, 0.0)
    weights = weights + jnp.where(step == -1, 8.0, 0.0) - jnp.where(step == 1, 8.0, 0.0)
    band[...] = weights.astype(BF16)

    def inner_z(pair):
        cols = pl.ds(pl.multiple_of(pair * wide, wide), wide)
        parts = [
            jnp.concatenate([ref[f, first:first + N, cols] for f in range(3)], axis=0)
            for ref, first in ((halves, 0), (halves, N), (thirds, 0))
        ]
        out = lax.dot_general(
            jnp.concatenate(parts, axis=1), band[...], (((1,), (0,)), ((), ())), preferred_element_type=F32
        )
        for f in range(3):
            for r in range(2):
                dz_buf[f, 2 * pair + r] = out[f * N:(f + 1) * N, r * RZ:(r + 1) * RZ]

    def derivative(m2, m1, p1, p2):
        return 8.0 * (p1 - m1) + (m2 - p2)

    def without_z(row):
        for b in range(N // XB):
            at = XC + b * XB

            def dx(f):
                return derivative(*(fld[f, row + 2, pl.ds(at + k, XB), :] for k in (-2, -1, 1, 2)))

            def dy(f):
                return derivative(*(fld[f, row + 2 + k, pl.ds(at, XB), :] for k in (-2, -1, 1, 2)))

            here = pl.ds(b * XB, XB)
            dxu, dxv, dyu, dyv = dx(0), dx(1), dy(0), dy(1)
            rotation, shear = dxv - dyu, dxv + dyu
            enst[row, here, :] = rotation * rotation
            strn[row, here, :] = 2.0 * (dxu * dxu + dyv * dyv) + shear * shear
            dxw_buf[row, here, :] = dx(2)
            dyw_buf[row, here, :] = dy(2)

    outer = (lane < 2) | (lane >= RZ - 2)

    def with_z(row):
        cols = pl.ds(pl.multiple_of(row * RZ, RZ), RZ)
        for b in range(N // XB):
            here = pl.ds(b * XB, XB)

            def dz(f):
                shift = lax.rem(RZ + RZ - 2 - 4 * lax.rem(f * RY + row, 32), RZ)
                edge = pltpu.roll(edges[0 if f < 2 else 1, here, :], shift, 1)
                return dz_buf[f, row, here, :] + jnp.where(outer, edge, 0.0)

            dzu, dzv, dzw = dz(0), dz(1), dz(2)
            dxw, dyw = dxw_buf[row, here, :], dyw_buf[row, here, :]
            r1, r2, s1, s2 = dxw - dzu, dyw - dzv, dxw + dzu, dyw + dzv
            e = (enst[row, here, :] + r1 * r1 + r2 * r2) * (1.0 / 288.0)
            s = (strn[row, here, :] + 2.0 * dzw * dzw + s1 * s1 + s2 * s2) * (1.0 / 288.0)
            enst[row, here, :] = e
            strn[row, here, :] = s
            for q, value in ((3, e), (4, s)):
                high = value.astype(BF16)
                halves[q, here, cols] = high
                halves[q, pl.ds(N + b * XB, XB), cols] = (value - high.astype(F32)).astype(BF16)

    def inner_pair(pair, carry):
        inner_z(pair)
        without_z(2 * pair)
        without_z(2 * pair + 1)
        return carry

    def face_pair(i, carry):
        inner_z(i * (RY // 2 - 1))
        return carry

    lax.fori_loop(1, RY // 2 - 1, inner_pair, 0)
    lax.fori_loop(0, 2, face_pair, 0)
    for cp in z_halo:
        cp.wait_recv()

    def edge(b, carry):
        here = pl.ds(pl.multiple_of(b * XB, XB), XB)
        lo, hi = from_left[here, :], from_right[here, :]
        packs = (
            jnp.where(low_half, lo, pltpu.roll(hi, 2, 1)),
            jnp.where(low_half, pltpu.roll(lo, RZ - 2, 1), hi),
        )
        for k, m in enumerate(packs):
            next2, next1 = pltpu.roll(m, RZ - 2, 1), pltpu.roll(m, RZ - 1, 1)
            last1, last2 = pltpu.roll(m, 1, 1), pltpu.roll(m, 2, 1)
            tops = jnp.where(member == 0, -next2, 8.0 * next1 - next2)
            bottoms = jnp.where(member == 2, last2 - 8.0 * last1, last2)
            edges[k, here, :] = jnp.where(low_half, tops, bottoms)
        return carry

    lax.fori_loop(0, N // XB, edge, 0)

    def inner_row(row, carry):
        with_z(row)
        return carry

    lax.fori_loop(2, RY - 2, inner_row, 0)
    inside = pl.ds(2 * RZ, (RY - 4) * RZ)
    for q in range(2):
        grams[q] = gram(3 + q, inside)

    def face(which):
        first = (RY - 2) * which
        for r in range(2):
            y_copy(which, r).wait_recv()

        def face_row(r, carry):
            without_z(first + r)
            with_z(first + r)
            return carry

        lax.fori_loop(0, 2, face_row, 0)
        cols = pl.ds(pl.multiple_of(first * RZ, wide), wide)
        for q in range(2):
            grams[q] = grams[q] + gram(3 + q, cols)

    def one_face(i, carry):
        face(lax.rem(i + 1 + c, CORES))
        return carry

    lax.fori_loop(0, 2, one_face, 0)

    ge, gs = grams[0], grams[1]
    fill(late.piece, [jnp.where(below, ge, gs)], [diagonal(ge), diagonal(gs)])
    late.scatter()
    early.along_y()
    late.along_y()
    early.along_z()
    late.along_z()
    first_sums = early.total()
    last_sums = late.total()

    diag = jnp.concatenate(
        [first_sums[2 * own_rows:2 * own_rows + 3, :], last_sums[own_rows:own_rows + 5, :]], axis=0
    )
    trace = jnp.sum(diag, axis=1, keepdims=True)
    weight = 1.0 / (5.0 * cells * (trace / (N * cells) + 1e-6))
    wide_weights = [jnp.broadcast_to(weight[q:q + 1, :], (own_rows, N)) for q in range(5)]
    row_id = me * own_rows + lax.broadcasted_iota(jnp.int32, (own_rows, N), 0)
    lower = row_id > lax.broadcasted_iota(jnp.int32, (own_rows, N), 1)
    mine = pl.ds(pl.multiple_of(me * own_rows, own_rows), own_rows)
    comb[mine, :] = (
        first_sums[:own_rows, :] * jnp.where(lower, wide_weights[0], wide_weights[1])
        + first_sums[own_rows:2 * own_rows, :] * jnp.where(lower, wide_weights[2], 0.0)
        + last_sums[:own_rows, :] * jnp.where(lower, wide_weights[3], wide_weights[4])
    )
    ag = [remote(comb.at[mine, :], comb.at[mine, :], ag_send.at[k], ag_recv.at[k], to) for k, _, to in rs_peers]
    for cp in ag:
        cp.start()
    for cp in sends + early.rs + early.ey + early.ez + late.rs + late.ey + late.ez:
        cp.wait_send()
    five = lax.broadcasted_iota(jnp.int32, diag.shape, 0) < 5
    middle = jnp.sum(jnp.where(five, diag * weight, 0.0), axis=0, keepdims=True)
    for cp in ag:
        cp.wait_recv()
    square = comb[...]
    half = jnp.where(below, square, 0.0) + jnp.where(below, square.T, 0.0)
    cross_out[...] = half + half.T + jnp.where(eye, jnp.broadcast_to(middle, (N, N)), 0.0)
    for cp in ag:
        cp.wait_send()


def split3(v):
    high = v.astype(BF16).astype(F32)
    rest = v - high
    middle = rest.astype(BF16).astype(F32)
    return high, middle, rest - middle


def factor_kernel(cross, e_in, s_in, e_out, s_out, factor, work, upper, out_sem):
    stores = [
        pltpu.make_async_copy(src.at[r], dst.at[:, r, :], out_sem.at[q, r])
        for q, (src, dst) in enumerate(((e_in, e_out), (s_in, s_out)))
        for r in range(RY)
    ]
    for cp in stores:
        cp.start()
    work[...] = cross[...]
    lane = lax.broadcasted_iota(jnp.int32, (8, N), 1)
    sub = lax.broadcasted_iota(jnp.int32, (8, N), 0)
    for p in range(N // 8):
        base = 8 * p
        v = work[base:base + 8, :]
        rows = [jnp.broadcast_to(v[k:k + 1, :], (8, N)) for k in range(8)]
        s = {}
        for k in range(8):
            for m in range(k, 8):
                s[k, m] = jnp.broadcast_to(rows[k][:, base + m:base + m + 1], (8, N))
        panel = None
        for k in range(8):
            r = lax.rsqrt(s[k, k])
            u = {m: s[k, m] * r for m in range(k + 1, 8)}
            for m in range(k + 1, 8):
                for q in range(m, 8):
                    s[m, q] = s[m, q] - u[m] * u[q]
            rows[k] = rows[k] * r
            for m in range(k + 1, 8):
                rows[m] = rows[m] - u[m] * rows[k]
            panel = rows[k] if panel is None else jnp.where(sub == k, rows[k], panel)
        upper[base:base + 8, :] = jnp.where(lane >= sub + base, panel, 0.0)
        if p < N // 8 - 1:
            hi, mid, lo = split3(panel)
            lhs = jnp.concatenate([hi, hi, mid, mid, hi, lo], axis=0).astype(BF16)
            rhs = jnp.concatenate([hi, mid, hi, mid, lo, hi], axis=0).astype(BF16)
            update = lax.dot_general(lhs, rhs, (((0,), (0,)), ((), ())), preferred_element_type=F32)
            work[base + 8:, :] = work[base + 8:, :] - update[base + 8:, :]
    factor[...] = upper[...].T
    for cp in stores:
        cp.wait()


def per_device(sizes, fields):
    gy, gz, zc = sizes
    yc, xc = gy // CORES, gz // zc
    owners = xc * CORES
    vmem = pl.BlockSpec(memory_space=pltpu.VMEM)
    anywhere = pl.BlockSpec(memory_space=pl.ANY)
    grid_rows = jax.ShapeDtypeStruct((RY, N, RZ), F32)
    dma = pltpu.SemaphoreType.DMA

    def body(*refs):
        main_kernel(sizes, *refs)

    def channel(squares):
        rows = squares * (N // owners) + 8
        return [
            pltpu.VMEM((owners, rows, N), F32),
            pltpu.VMEM((owners - 1, rows, N), F32),
            pltpu.VMEM((rows, N), F32),
            pltpu.VMEM((yc - 1, rows, N), F32),
            pltpu.VMEM((rows, N), F32),
            pltpu.VMEM((zc - 1, rows, N), F32),
            dma((owners - 1,)),
            dma((owners - 1,)),
            dma((yc - 1,)),
            dma((yc - 1,)),
            dma((zc - 1,)),
            dma((zc - 1,)),
        ]

    e, s, cross = pl.pallas_call(
        body,
        out_shape=(grid_rows, grid_rows, jax.ShapeDtypeStruct((N, N), F32)),
        in_specs=[pl.BlockSpec(memory_space=pltpu.HBM)],
        out_specs=(vmem, vmem, vmem),
        scratch_shapes=[
            pltpu.VMEM((3, RY + 4, N + 16, RZ), F32),
            pltpu.VMEM((N, RZ), F32),
            pltpu.VMEM((N, RZ), F32),
            pltpu.VMEM((N, RZ), F32),
            pltpu.VMEM((N, RZ), F32),
            pltpu.VMEM((2, N, RZ), F32),
            pltpu.VMEM((3, RY, N, RZ), F32),
            pltpu.VMEM((RY, N, RZ), F32),
            pltpu.VMEM((RY, N, RZ), F32),
            pltpu.VMEM((5, 2 * N, RY * RZ), BF16),
            pltpu.VMEM((3, N, RY * RZ), BF16),
            pltpu.VMEM((6 * RZ, 2 * RZ), BF16),
            pltpu.VMEM((2, N, N), F32),
            pltpu.VMEM((N, N), F32),
            dma((RY,)),
            dma((6,)),
            dma((6,)),
            dma((owners - 1,)),
            dma((owners - 1,)),
            *channel(2),
            *channel(1),
        ],
        compiler_params=pltpu.CompilerParams(collective_id=0, has_side_effects=True, vmem_limit_bytes=48 << 20),
        name="stencil_gram",
    )(pltpu.with_memory_space_constraint(fields, pltpu.HBM))
    whole = jax.ShapeDtypeStruct((N, RY, RZ), F32)
    return pl.pallas_call(
        factor_kernel,
        out_shape=(whole, whole, jax.ShapeDtypeStruct((N, N), F32)),
        in_specs=[vmem, vmem, vmem],
        out_specs=(anywhere, anywhere, vmem),
        scratch_shapes=[
            pltpu.VMEM((N, N), F32),
            pltpu.VMEM((N, N), F32),
            dma((2, RY)),
        ],
        compiler_params=pltpu.CompilerParams(vmem_limit_bytes=16 << 20),
        name="factor",
    )(cross, e, s)


def solution(mesh):
    gy, gz = mesh.shape["gy"], mesh.shape["gz"]
    sizes = (gy, gz, 8 if gz % 8 == 0 else 2)

    def call(fields):
        return per_device(sizes, fields)

    return jax.shard_map(
        call,
        mesh=mesh,
        in_specs=(P(None, None, "gy", "gz"),),
        out_specs=(P(None, "gy", "gz"), P(None, "gy", "gz"), P()),
        check_vma=False,
    )
```

time: 69.2 us -> 55.7 us (0.80)
  Pallas kernels: 68.4 us -> 54.9 us
    pallas_call x1, Pallas kernels: 60.5 us -> 47 us  [per_device(): pl.pallas_call(body, out_shape=(grid_rows, grid_rows, jax.ShapeDtypeStruc...]
where the time goes in v2:
time: 55.7 us; the launch traced here: 55.5 us
  Pallas kernels  54.9 us (99%)
  between operations  0.64 us (1%)
    pallas_call x1, Pallas kernels, per_device(): pl.pallas_call(body, out_shape=(grid_rows, grid_rows, jax.ShapeDtypeStruc...  47 us
    pallas_call x1, Pallas kernels, per_device(): pl.pallas_call(factor_kernel, out_shape=(whole, whole, jax.ShapeDtypeStru...  7.91 us

profile of v2, /device:TPU:1, one launch (start us, length us, event | category | flops | bytes accessed | tf_op | source)
XLA Modules:
  0.0 55.5 jit_solution(8567969810582712303)
XLA Ops:
  0.6 47.0 %stencil_gram.1 = (f32[16,128,128]{2,1,0:T(8,128)S(1)}, f32[16,128,128]{2,1,0:T(8,128)S(1)}, f32[128,128]{1,0:T(8,128)S(1)}) custom-call(f32[3,132,16,128]{3,2,1,0:T(8,128)} %refs_0_.1), custom_call_target="tpu_custom_call" | custom-call | tf_op jit(solution)/shard_map/stencil_gram/pallas_call | solution.py:464
  47.6 7.9 %factor.1 = (f32[128,16,128]{2,1,0:T(8,128)}, f32[128,16,128]{2,1,0:T(8,128)}, f32[128,128]{1,0:T(8,128)}) custom-call(f32[128,128]{1,0:T(8,128)S(1)} %get-tuple-element.6.cross, f32[16,128,128]{2,1,0:T(8,128)S(1)} %get-tuple-element.7.e_in, f32[16,128,128]{2,1,0:T(8,128)S(1)} %get-tuple-element.8.s_in), custom_call_target="tpu_custom_call" | custom-call | tf_op jit(solution)/shard_map/factor/pallas_call | solution.py:496

commit v3 on v2

--- a/solution.py
+++ b/solution.py
@@ -13,6 +13,7 @@
 X0 = 6
 XC = X0 + 2
 XB = 16
+PARTS = 2
 F32 = jnp.float32
 BF16 = jnp.bfloat16
 
@@ -170,7 +171,7 @@
         return jnp.sum(jnp.where(eye, m, 0.0), axis=0, keepdims=True)
 
     def fill(piece, squares, diags):
-        tail = jnp.concatenate(diags + [jnp.zeros((8 - len(diags), N), F32)], axis=0)
+        tail = jnp.concatenate(diags, axis=0)
         for o in range(owners):
             for k, value in enumerate(squares):
                 piece[o, k * own_rows:(k + 1) * own_rows, :] = value[o * own_rows:(o + 1) * own_rows, :]
@@ -216,31 +217,35 @@
     early.scatter()
 
     wide = 2 * RZ
-    depth = lax.broadcasted_iota(jnp.int32, (3 * wide, wide), 0) % wide
-    column = lax.broadcasted_iota(jnp.int32, (3 * wide, wide), 1)
-    step = jnp.where(depth // RZ == column // RZ, column - depth, 0)
-    weights = jnp.where(step == 2, 1.0, 0.0) - jnp.where(step == -2, 1.0, 0.0)
-    weights = weights + jnp.where(step == -1, 8.0, 0.0) - jnp.where(step == 1, 8.0, 0.0)
-    band[...] = weights.astype(BF16)
-
-    def inner_z(pair):
+    step = lax.broadcasted_iota(jnp.int32, (RZ, RZ), 1) - lax.broadcasted_iota(jnp.int32, (RZ, RZ), 0)
+    weights = jnp.where(step == 2, 1.0, jnp.where(step == -2, -1.0, 0.0))
+    weights = jnp.where(step == -1, 8.0, jnp.where(step == 1, -8.0, weights)).astype(BF16)
+    band[...] = jnp.zeros_like(band)
+    band[:RZ, :RZ] = weights
+    band[RZ:, RZ:] = weights
+
+    def inner_z(pair, part):
+        rows = N // PARTS
         cols = pl.ds(pl.multiple_of(pair * wide, wide), wide)
+        at = part * rows
         parts = [
-            jnp.concatenate([ref[f, first:first + N, cols] for f in range(3)], axis=0)
+            ref[f, pl.ds(first + at, rows), cols]
             for ref, first in ((halves, 0), (halves, N), (thirds, 0))
+            for f in range(3)
         ]
         out = lax.dot_general(
-            jnp.concatenate(parts, axis=1), band[...], (((1,), (0,)), ((), ())), preferred_element_type=F32
+            jnp.concatenate(parts, axis=0), band[...], (((1,), (0,)), ((), ())), preferred_element_type=F32
         )
         for f in range(3):
             for r in range(2):
-                dz_buf[f, 2 * pair + r] = out[f * N:(f + 1) * N, r * RZ:(r + 1) * RZ]
+                a, b, c2 = (out[(3 * k + f) * rows:(3 * k + f + 1) * rows, r * RZ:(r + 1) * RZ] for k in range(3))
+                dz_buf[f, 2 * pair + r, pl.ds(at, rows), :] = a + b + c2
 
     def derivative(m2, m1, p1, p2):
         return 8.0 * (p1 - m1) + (m2 - p2)
 
-    def without_z(row):
-        for b in range(N // XB):
+    def without_z(row, blocks=range(N // XB)):
+        for b in blocks:
             at = XC + b * XB
 
             def dx(f):
@@ -282,13 +287,16 @@
                 halves[q, pl.ds(N + b * XB, XB), cols] = (value - high.astype(F32)).astype(BF16)
 
     def inner_pair(pair, carry):
-        inner_z(pair)
-        without_z(2 * pair)
-        without_z(2 * pair + 1)
+        each = N // XB // PARTS
+        for part in range(PARTS):
+            inner_z(pair, part)
+            for r in range(2):
+                without_z(2 * pair + r, range(part * each, (part + 1) * each))
         return carry
 
     def face_pair(i, carry):
-        inner_z(i * (RY // 2 - 1))
+        for part in range(PARTS):
+            inner_z(i * (RY // 2 - 1), part)
         return carry
 
     lax.fori_loop(1, RY // 2 - 1, inner_pair, 0)
@@ -313,11 +321,12 @@
 
     lax.fori_loop(0, N // XB, edge, 0)
 
-    def inner_row(row, carry):
-        with_z(row)
-        return carry
-
-    lax.fori_loop(2, RY - 2, inner_row, 0)
+    def inner_rows(pair, carry):
+        with_z(2 * pair)
+        with_z(2 * pair + 1)
+        return carry
+
+    lax.fori_loop(1, RY // 2 - 1, inner_rows, 0)
     inside = pl.ds(2 * RZ, (RY - 4) * RZ)
     for q in range(2):
         grams[q] = gram(3 + q, inside)
@@ -337,25 +346,20 @@
         for q in range(2):
             grams[q] = grams[q] + gram(3 + q, cols)
 
-    def one_face(i, carry):
-        face(lax.rem(i + 1 + c, CORES))
-        return carry
-
-    lax.fori_loop(0, 2, one_face, 0)
+    face(lax.rem(1 + c, CORES))
+    early.along_y()
+    face(c)
 
     ge, gs = grams[0], grams[1]
     fill(late.piece, [jnp.where(below, ge, gs)], [diagonal(ge), diagonal(gs)])
     late.scatter()
-    early.along_y()
     late.along_y()
     early.along_z()
     late.along_z()
     first_sums = early.total()
     last_sums = late.total()
 
-    diag = jnp.concatenate(
-        [first_sums[2 * own_rows:2 * own_rows + 3, :], last_sums[own_rows:own_rows + 5, :]], axis=0
-    )
+    diag = jnp.concatenate([first_sums[2 * own_rows:, :], last_sums[own_rows:, :]], axis=0)
     trace = jnp.sum(diag, axis=1, keepdims=True)
     weight = 1.0 / (5.0 * cells * (trace / (N * cells) + 1e-6))
     wide_weights = [jnp.broadcast_to(weight[q:q + 1, :], (own_rows, N)) for q in range(5)]
@@ -372,8 +376,7 @@
         cp.start()
     for cp in sends + early.rs + early.ey + early.ez + late.rs + late.ey + late.ez:
         cp.wait_send()
-    five = lax.broadcasted_iota(jnp.int32, diag.shape, 0) < 5
-    middle = jnp.sum(jnp.where(five, diag * weight, 0.0), axis=0, keepdims=True)
+    middle = jnp.sum(diag * weight, axis=0, keepdims=True)
     for cp in ag:
         cp.wait_recv()
     square = comb[...]
@@ -444,8 +447,8 @@
     def body(*refs):
         main_kernel(sizes, *refs)
 
-    def channel(squares):
-        rows = squares * (N // owners) + 8
+    def channel(squares, diags):
+        rows = squares * (N // owners) + diags
         return [
             pltpu.VMEM((owners, rows, N), F32),
             pltpu.VMEM((owners - 1, rows, N), F32),
@@ -478,7 +481,7 @@
             pltpu.VMEM((RY, N, RZ), F32),
             pltpu.VMEM((5, 2 * N, RY * RZ), BF16),
             pltpu.VMEM((3, N, RY * RZ), BF16),
-            pltpu.VMEM((6 * RZ, 2 * RZ), BF16),
+            pltpu.VMEM((2 * RZ, 2 * RZ), BF16),
             pltpu.VMEM((2, N, N), F32),
             pltpu.VMEM((N, N), F32),
             dma((RY,)),
@@ -486,8 +489,8 @@
             dma((6,)),
             dma((owners - 1,)),
             dma((owners - 1,)),
-            *channel(2),
-            *channel(1),
+            *channel(2, 3),
+            *channel(1, 2),
         ],
         compiler_params=pltpu.CompilerParams(collective_id=0, has_side_effects=True, vmem_limit_bytes=48 << 20),
         name="stencil_gram",

time: 55.7 us -> 54.5 us (0.978)
  Pallas kernels: 54.9 us -> 53.7 us
    pallas_call x1, Pallas kernels: 47 us -> 45.8 us  [per_device(): pl.pallas_call(body, out_shape=(grid_rows, grid_rows, jax.ShapeDtypeStruc...]
where the time goes in v3:
time: 54.5 us; the launch traced here: 54.4 us
  Pallas kernels  53.7 us (99%)
  between operations  0.64 us (1%)
    pallas_call x1, Pallas kernels, per_device(): pl.pallas_call(body, out_shape=(grid_rows, grid_rows, jax.ShapeDtypeStruc...  45.8 us
    pallas_call x1, Pallas kernels, per_device(): pl.pallas_call(factor_kernel, out_shape=(whole, whole, jax.ShapeDtypeStru...  7.91 us

profile of v3, /device:TPU:1, one launch (start us, length us, event | category | flops | bytes accessed | tf_op | source)
XLA Modules:
  0.0 54.4 jit_solution(2100543699340580051)
XLA Ops:
  0.6 45.8 %stencil_gram.1 = (f32[16,128,128]{2,1,0:T(8,128)S(1)}, f32[16,128,128]{2,1,0:T(8,128)S(1)}, f32[128,128]{1,0:T(8,128)S(1)}) custom-call(f32[3,132,16,128]{3,2,1,0:T(8,128)} %refs_0_.1), custom_call_target="tpu_custom_call" | custom-call | tf_op jit(solution)/shard_map/stencil_gram/pallas_call | solution.py:467
  46.4 7.9 %factor.1 = (f32[128,16,128]{2,1,0:T(8,128)}, f32[128,16,128]{2,1,0:T(8,128)}, f32[128,128]{1,0:T(8,128)}) custom-call(f32[128,128]{1,0:T(8,128)S(1)} %get-tuple-element.6.cross, f32[16,128,128]{2,1,0:T(8,128)S(1)} %get-tuple-element.7.e_in, f32[16,128,128]{2,1,0:T(8,128)S(1)} %get-tuple-element.8.s_in), custom_call_target="tpu_custom_call" | custom-call | tf_op jit(solution)/shard_map/factor/pallas_call | solution.py:499

commit v4 on v3

--- a/solution.py
+++ b/solution.py
@@ -29,6 +29,7 @@
     strn,
     cross_out,
     fld,
+    packs,
     pack_r,
     pack_l,
     from_left,
@@ -87,6 +88,7 @@
     peers = [p for _, p in ey_peers + ez_peers] + [p for _, _, p in rs_peers] + [up, down, right, left]
     for p in peers:
         pl.semaphore_signal(barrier, inc=1, device_id=p, device_id_type=MESH)
+    packs[...] = jnp.zeros_like(packs)
     for row in faces:
         load(row).wait()
     pl.semaphore_wait(barrier, len(peers))
@@ -111,14 +113,27 @@
         middle = rest.astype(BF16)
         return high, middle, (rest - middle.astype(F32)).astype(BF16)
 
+    lane = lax.broadcasted_iota(jnp.int32, (XB, RZ), 1)
+    group = lane // 4
+    member = lane % 4
+    low_half = member < 2
+
     def split_fields(row):
         cols = pl.ds(pl.multiple_of(row * RZ, RZ), RZ)
-        for f in range(3):
-            for b in range(N // XB):
-                high, middle, low = three_way(fld[f, row + 2, pl.ds(XC + b * XB, XB), :])
-                halves[f, pl.ds(b * XB, XB), cols] = high
+        places = [lax.rem(f * RY + row, 32) for f in range(3)]
+        for b in range(N // XB):
+            here = pl.ds(b * XB, XB)
+            faces_here = []
+            for f in range(3):
+                value = fld[f, row + 2, pl.ds(XC + b * XB, XB), :]
+                faces_here.append(pltpu.roll(value, lax.rem(4 * places[f] + 2, RZ), 1))
+                high, middle, low = three_way(value)
+                halves[f, here, cols] = high
                 halves[f, pl.ds(N + b * XB, XB), cols] = middle
-                thirds[f, pl.ds(b * XB, XB), cols] = low
+                thirds[f, here, cols] = low
+            first = jnp.where(group == places[0], faces_here[0], packs[0, here, :])
+            packs[0, here, :] = jnp.where(group == places[1], faces_here[1], first)
+            packs[1, here, :] = jnp.where(group == places[2], faces_here[2], packs[1, here, :])
 
     def split_face(i, carry):
         split_fields(i + (RY - 4) * (i // 2))
@@ -132,25 +147,11 @@
     lax.fori_loop(0, 4, split_face, 0)
     lax.fori_loop(2, RY - 2, split_rest, 0)
 
-    lane = lax.broadcasted_iota(jnp.int32, (XB, RZ), 1)
-    group = lane // 4
-    member = lane % 4
-    low_half = member < 2
-
-    def pack(b, carry):
-        row = pl.multiple_of(XC + b * XB, 8)
-        packs = [jnp.zeros((XB, RZ), F32) for _ in range(2)]
-        for t in range(3 * RY):
-            j = t % 32
-            v = fld[t // RY, t % RY + 2, pl.ds(row, XB), :]
-            v = pltpu.roll(v, (4 * j + 2) % RZ, 1)
-            packs[t // 32] = jnp.where(group == j, v, packs[t // 32])
-        out = pl.ds(pl.multiple_of(b * XB, XB), XB)
-        pack_r[out, :] = jnp.where(low_half, packs[0], pltpu.roll(packs[1], 2, 1))
-        pack_l[out, :] = jnp.where(low_half, pltpu.roll(packs[0], RZ - 2, 1), packs[1])
-        return carry
-
-    lax.fori_loop(0, N // XB, pack, 0)
+    for b in range(N // XB):
+        here = pl.ds(b * XB, XB)
+        lo, hi = packs[0, here, :], packs[1, here, :]
+        pack_r[here, :] = jnp.where(low_half, lo, pltpu.roll(hi, 2, 1))
+        pack_l[here, :] = jnp.where(low_half, pltpu.roll(lo, RZ - 2, 1), hi)
     z_halo = [
         remote(pack_r, from_left, halo_send.at[4], halo_recv.at[4], right),
         remote(pack_l, from_right, halo_send.at[5], halo_recv.at[5], left),
@@ -307,11 +308,11 @@
     def edge(b, carry):
         here = pl.ds(pl.multiple_of(b * XB, XB), XB)
         lo, hi = from_left[here, :], from_right[here, :]
-        packs = (
+        joined = (
             jnp.where(low_half, lo, pltpu.roll(hi, 2, 1)),
             jnp.where(low_half, pltpu.roll(lo, RZ - 2, 1), hi),
         )
-        for k, m in enumerate(packs):
+        for k, m in enumerate(joined):
             next2, next1 = pltpu.roll(m, RZ - 2, 1), pltpu.roll(m, RZ - 1, 1)
             last1, last2 = pltpu.roll(m, 1, 1), pltpu.roll(m, 2, 1)
             tops = jnp.where(member == 0, -next2, 8.0 * next1 - next2)
@@ -379,21 +380,13 @@
     middle = jnp.sum(diag * weight, axis=0, keepdims=True)
     for cp in ag:
         cp.wait_recv()
-    square = comb[...]
-    half = jnp.where(below, square, 0.0) + jnp.where(below, square.T, 0.0)
-    cross_out[...] = half + half.T + jnp.where(eye, jnp.broadcast_to(middle, (N, N)), 0.0)
+    square = jnp.where(eye, 0.0, comb[...])
+    cross_out[...] = square + square.T + jnp.where(eye, jnp.broadcast_to(middle, (N, N)), 0.0)
     for cp in ag:
         cp.wait_send()
 
 
-def split3(v):
-    high = v.astype(BF16).astype(F32)
-    rest = v - high
-    middle = rest.astype(BF16).astype(F32)
-    return high, middle, rest - middle
-
-
-def factor_kernel(cross, e_in, s_in, e_out, s_out, factor, work, upper, out_sem):
+def factor_kernel(cross, e_in, s_in, e_out, s_out, factor, upper, spread, out_sem):
     stores = [
         pltpu.make_async_copy(src.at[r], dst.at[:, r, :], out_sem.at[q, r])
         for q, (src, dst) in enumerate(((e_in, e_out), (s_in, s_out)))
@@ -401,35 +394,46 @@
     ]
     for cp in stores:
         cp.start()
-    work[...] = cross[...]
     lane = lax.broadcasted_iota(jnp.int32, (8, N), 1)
     sub = lax.broadcasted_iota(jnp.int32, (8, N), 0)
-    for p in range(N // 8):
+    count = N // 8
+    blocks = [cross[8 * i:8 * i + 8, :] for i in range(count)]
+    for p in range(count):
         base = 8 * p
-        v = work[base:base + 8, :]
+        v = blocks[p]
         rows = [jnp.broadcast_to(v[k:k + 1, :], (8, N)) for k in range(8)]
-        s = {}
+        for m in range(8):
+            spread[m] = jnp.broadcast_to(v[:, base + m:base + m + 1], (8, N))
+        s = {(k, m): spread[m, pl.ds(k, 8, stride=0), :] for m in range(8) for k in range(m + 1)}
+        columns = {
+            (i, k): jnp.broadcast_to(blocks[i][:, base + k:base + k + 1], (8, N))
+            for i in range(p + 1, count)
+            for k in range(8)
+        }
+        inverse, u, panel = [], {}, None
         for k in range(8):
-            for m in range(k, 8):
-                s[k, m] = jnp.broadcast_to(rows[k][:, base + m:base + m + 1], (8, N))
-        panel = None
-        for k in range(8):
-            r = lax.rsqrt(s[k, k])
-            u = {m: s[k, m] * r for m in range(k + 1, 8)}
+            inverse.append(lax.rsqrt(s[k, k]))
+            for m in range(k + 1, 8):
+                u[k, m] = s[k, m] * inverse[k]
             for m in range(k + 1, 8):
                 for q in range(m, 8):
-                    s[m, q] = s[m, q] - u[m] * u[q]
-            rows[k] = rows[k] * r
+                    s[m, q] = s[m, q] - u[k, m] * u[k, q]
+            rows[k] = rows[k] * inverse[k]
             for m in range(k + 1, 8):
-                rows[m] = rows[m] - u[m] * rows[k]
+                rows[m] = rows[m] - u[k, m] * rows[k]
             panel = rows[k] if panel is None else jnp.where(sub == k, rows[k], panel)
         upper[base:base + 8, :] = jnp.where(lane >= sub + base, panel, 0.0)
-        if p < N // 8 - 1:
-            hi, mid, lo = split3(panel)
-            lhs = jnp.concatenate([hi, hi, mid, mid, hi, lo], axis=0).astype(BF16)
-            rhs = jnp.concatenate([hi, mid, hi, mid, lo, hi], axis=0).astype(BF16)
-            update = lax.dot_general(lhs, rhs, (((0,), (0,)), ((), ())), preferred_element_type=F32)
-            work[base + 8:, :] = work[base + 8:, :] - update[base + 8:, :]
+        if p == count - 1:
+            break
+        for k in range(7, -1, -1):
+            rows[k] = rows[k] * inverse[k]
+            for m in range(k):
+                rows[m] = rows[m] - u[m, k] * rows[k]
+        for i in range(p + 1, count):
+            terms = [columns[i, k] * rows[k] for k in range(8)]
+            while len(terms) > 1:
+                terms = [terms[t] + terms[t + 1] for t in range(0, len(terms), 2)]
+            blocks[i] = blocks[i] - terms[0]
     factor[...] = upper[...].T
     for cp in stores:
         cp.wait()
@@ -471,6 +475,7 @@
         out_specs=(vmem, vmem, vmem),
         scratch_shapes=[
             pltpu.VMEM((3, RY + 4, N + 16, RZ), F32),
+            pltpu.VMEM((2, N, RZ), F32),
             pltpu.VMEM((N, RZ), F32),
             pltpu.VMEM((N, RZ), F32),
             pltpu.VMEM((N, RZ), F32),
@@ -503,7 +508,7 @@
         out_specs=(anywhere, anywhere, vmem),
         scratch_shapes=[
             pltpu.VMEM((N, N), F32),
-            pltpu.VMEM((N, N), F32),
+            pltpu.VMEM((8, 8, N), F32),
             dma((2, RY)),
         ],
         compiler_params=pltpu.CompilerParams(vmem_limit_bytes=16 << 20),

time: 54.5 us -> 50.8 us (0.932)
  Pallas kernels: 53.7 us -> 50.1 us
    pallas_call x1, Pallas kernels: 7.91 us -> 5.04 us  [per_device(): pl.pallas_call(factor_kernel, out_shape=(whole, whole, jax.ShapeDtypeStru...]
    pallas_call x1, Pallas kernels: 45.8 us -> 45 us  [per_device(): pl.pallas_call(body, out_shape=(grid_rows, grid_rows, jax.ShapeDtypeStruc...]
where the time goes in v4:
time: 50.8 us; the launch traced here: 50.7 us
  Pallas kernels  50.1 us (99%)
  between operations  0.64 us (1%)
    pallas_call x1, Pallas kernels, per_device(): pl.pallas_call(body, out_shape=(grid_rows, grid_rows, jax.ShapeDtypeStruc...  45 us
    pallas_call x1, Pallas kernels, per_device(): pl.pallas_call(factor_kernel, out_shape=(whole, whole, jax.ShapeDtypeStru...  5.04 us

profile of v4, /device:TPU:1, one launch (start us, length us, event | category | flops | bytes accessed | tf_op | source)
XLA Modules:
  0.0 50.7 jit_solution(11578992536101494875)
XLA Ops:
  0.6 45.0 %stencil_gram.1 = (f32[16,128,128]{2,1,0:T(8,128)S(1)}, f32[16,128,128]{2,1,0:T(8,128)S(1)}, f32[128,128]{1,0:T(8,128)S(1)}) custom-call(f32[3,132,16,128]{3,2,1,0:T(8,128)} %refs_0_.1), custom_call_target="tpu_custom_call" | custom-call | tf_op jit(solution)/shard_map/stencil_gram/pallas_call | solution.py:471
  45.7 5.0 %factor.1 = (f32[128,16,128]{2,1,0:T(8,128)}, f32[128,16,128]{2,1,0:T(8,128)}, f32[128,128]{1,0:T(8,128)}) custom-call(f32[128,128]{1,0:T(8,128)S(1)} %get-tuple-element.6.cross, f32[16,128,128]{2,1,0:T(8,128)S(1)} %get-tuple-element.7.e_in, f32[16,128,128]{2,1,0:T(8,128)S(1)} %get-tuple-element.8.s_in), custom_call_target="tpu_custom_call" | custom-call | tf_op jit(solution)/shard_map/factor/pallas_call | solution.py:504

commit v5 on v4

--- a/solution.py
+++ b/solution.py
@@ -41,7 +41,6 @@
     halves,
     thirds,
     band,
-    grams,
     comb,
     load_sem,
     halo_send,
@@ -130,7 +129,8 @@
                 high, middle, low = three_way(value)
                 halves[f, here, cols] = high
                 halves[f, pl.ds(N + b * XB, XB), cols] = middle
-                thirds[f, here, cols] = low
+                if f < 2:
+                    thirds[f, here, cols] = low
             first = jnp.where(group == places[0], faces_here[0], packs[0, here, :])
             packs[0, here, :] = jnp.where(group == places[1], faces_here[1], first)
             packs[1, here, :] = jnp.where(group == places[2], faces_here[2], packs[1, here, :])
@@ -232,18 +232,23 @@
         parts = [
             ref[f, pl.ds(first + at, rows), cols]
             for ref, first in ((halves, 0), (halves, N), (thirds, 0))
-            for f in range(3)
+            for f in range(2)
         ]
         out = lax.dot_general(
             jnp.concatenate(parts, axis=0), band[...], (((1,), (0,)), ((), ())), preferred_element_type=F32
         )
-        for f in range(3):
+        for f in range(2):
             for r in range(2):
-                a, b, c2 = (out[(3 * k + f) * rows:(3 * k + f + 1) * rows, r * RZ:(r + 1) * RZ] for k in range(3))
+                a, b, c2 = (out[(2 * k + f) * rows:(2 * k + f + 1) * rows, r * RZ:(r + 1) * RZ] for k in range(3))
                 dz_buf[f, 2 * pair + r, pl.ds(at, rows), :] = a + b + c2
 
     def derivative(m2, m1, p1, p2):
         return 8.0 * (p1 - m1) + (m2 - p2)
+
+    def wrapped_z(row, blocks):
+        for b in blocks:
+            w = fld[2, row + 2, pl.ds(XC + b * XB, XB), :]
+            dz_buf[2, row, pl.ds(b * XB, XB), :] = derivative(*(pltpu.roll(w, k, 1) for k in (2, 1, RZ - 1, RZ - 2)))
 
     def without_z(row, blocks=range(N // XB)):
         for b in blocks:
@@ -266,12 +271,12 @@
     outer = (lane < 2) | (lane >= RZ - 2)
 
     def with_z(row):
-        cols = pl.ds(pl.multiple_of(row * RZ, RZ), RZ)
+        cols = pl.ds(row * RZ if isinstance(row, int) else pl.multiple_of(row * RZ, RZ), RZ)
         for b in range(N // XB):
             here = pl.ds(b * XB, XB)
 
             def dz(f):
-                shift = lax.rem(RZ + RZ - 2 - 4 * lax.rem(f * RY + row, 32), RZ)
+                shift = (2 * RZ - 2 - 4 * ((f * RY + row) % 32)) % RZ
                 edge = pltpu.roll(edges[0 if f < 2 else 1, here, :], shift, 1)
                 return dz_buf[f, row, here, :] + jnp.where(outer, edge, 0.0)
 
@@ -292,12 +297,17 @@
         for part in range(PARTS):
             inner_z(pair, part)
             for r in range(2):
-                without_z(2 * pair + r, range(part * each, (part + 1) * each))
+                blocks = range(part * each, (part + 1) * each)
+                wrapped_z(2 * pair + r, blocks)
+                without_z(2 * pair + r, blocks)
         return carry
 
     def face_pair(i, carry):
+        pair = i * (RY // 2 - 1)
         for part in range(PARTS):
-            inner_z(i * (RY // 2 - 1), part)
+            inner_z(pair, part)
+        for r in range(2):
+            wrapped_z(2 * pair + r, range(N // XB))
         return carry
 
     lax.fori_loop(1, RY // 2 - 1, inner_pair, 0)
@@ -312,7 +322,7 @@
             jnp.where(low_half, lo, pltpu.roll(hi, 2, 1)),
             jnp.where(low_half, pltpu.roll(lo, RZ - 2, 1), hi),
         )
-        for k, m in enumerate(joined):
+        for k, m in enumerate((joined[0], joined[1] - packs[1, here, :])):
             next2, next1 = pltpu.roll(m, RZ - 2, 1), pltpu.roll(m, RZ - 1, 1)
             last1, last2 = pltpu.roll(m, 1, 1), pltpu.roll(m, 2, 1)
             tops = jnp.where(member == 0, -next2, 8.0 * next1 - next2)
@@ -328,30 +338,18 @@
         return carry
 
     lax.fori_loop(1, RY // 2 - 1, inner_rows, 0)
-    inside = pl.ds(2 * RZ, (RY - 4) * RZ)
-    for q in range(2):
-        grams[q] = gram(3 + q, inside)
-
-    def face(which):
-        first = (RY - 2) * which
+    for way in range(2):
         for r in range(2):
-            y_copy(which, r).wait_recv()
-
-        def face_row(r, carry):
-            without_z(first + r)
-            with_z(first + r)
-            return carry
-
-        lax.fori_loop(0, 2, face_row, 0)
-        cols = pl.ds(pl.multiple_of(first * RZ, wide), wide)
-        for q in range(2):
-            grams[q] = grams[q] + gram(3 + q, cols)
-
-    face(lax.rem(1 + c, CORES))
+            y_copy(way, r).wait_recv()
     early.along_y()
-    face(c)
-
-    ge, gs = grams[0], grams[1]
+    inside = [gram(3 + q, pl.ds(wide, (RY - 4) * RZ)) for q in range(2)]
+    for row in faces:
+        without_z(row)
+        with_z(row)
+    ge, gs = (
+        inside[q] + gram(3 + q, pl.ds(0, wide)) + gram(3 + q, pl.ds((RY - 2) * RZ, wide)) for q in range(2)
+    )
+
     fill(late.piece, [jnp.where(below, ge, gs)], [diagonal(ge), diagonal(gs)])
     late.scatter()
     late.along_y()
@@ -403,7 +401,7 @@
         v = blocks[p]
         rows = [jnp.broadcast_to(v[k:k + 1, :], (8, N)) for k in range(8)]
         for m in range(8):
-            spread[m] = jnp.broadcast_to(v[:, base + m:base + m + 1], (8, N))
+            spread[m, 0:8, :] = jnp.broadcast_to(v[:, base + m:base + m + 1], (8, N))
         s = {(k, m): spread[m, pl.ds(k, 8, stride=0), :] for m in range(8) for k in range(m + 1)}
         columns = {
             (i, k): jnp.broadcast_to(blocks[i][:, base + k:base + k + 1], (8, N))
@@ -485,9 +483,8 @@
             pltpu.VMEM((RY, N, RZ), F32),
             pltpu.VMEM((RY, N, RZ), F32),
             pltpu.VMEM((5, 2 * N, RY * RZ), BF16),
-            pltpu.VMEM((3, N, RY * RZ), BF16),
+            pltpu.VMEM((2, N, RY * RZ), BF16),
             pltpu.VMEM((2 * RZ, 2 * RZ), BF16),
-            pltpu.VMEM((2, N, N), F32),
             pltpu.VMEM((N, N), F32),
             dma((RY,)),
             dma((6,)),
@@ -508,7 +505,7 @@
         out_specs=(anywhere, anywhere, vmem),
         scratch_shapes=[
             pltpu.VMEM((N, N), F32),
-            pltpu.VMEM((8, 8, N), F32),
+            pltpu.VMEM((8, 16, N), F32),
             dma((2, RY)),
         ],
         compiler_params=pltpu.CompilerParams(vmem_limit_bytes=16 << 20),

time: 50.8 us -> 49.8 us (0.980)
  Pallas kernels: 50.1 us -> 49.1 us
    pallas_call x1, Pallas kernels: 45 us -> 44 us  [per_device(): pl.pallas_call(body, out_shape=(grid_rows, grid_rows, jax.ShapeDtypeStruc...]
where the time goes in v5:
time: 49.8 us; the launch traced here: 49.7 us
  Pallas kernels  49.1 us (99%)
  between operations  0.64 us (1%)
    pallas_call x1, Pallas kernels, per_device(): pl.pallas_call(body, out_shape=(grid_rows, grid_rows, jax.ShapeDtypeStruc...  44 us
    pallas_call x1, Pallas kernels, per_device(): pl.pallas_call(factor_kernel, out_shape=(whole, whole, jax.ShapeDtypeStru...  5.04 us

profile of v5, /device:TPU:1, one launch (start us, length us, event | category | flops | bytes accessed | tf_op | source)
XLA Modules:
  0.0 49.7 jit_solution(14994733223722442374)
XLA Ops:
  0.6 44.0 %stencil_gram.1 = (f32[16,128,128]{2,1,0:T(8,128)S(1)}, f32[16,128,128]{2,1,0:T(8,128)S(1)}, f32[128,128]{1,0:T(8,128)S(1)}) custom-call(f32[3,132,16,128]{3,2,1,0:T(8,128)} %refs_0_.1), custom_call_target="tpu_custom_call" | custom-call | tf_op jit(solution)/shard_map/stencil_gram/pallas_call | solution.py:469
  44.7 5.0 %factor.1 = (f32[128,16,128]{2,1,0:T(8,128)}, f32[128,16,128]{2,1,0:T(8,128)}, f32[128,128]{1,0:T(8,128)}) custom-call(f32[128,128]{1,0:T(8,128)S(1)} %get-tuple-element.6.cross, f32[16,128,128]{2,1,0:T(8,128)S(1)} %get-tuple-element.7.e_in, f32[16,128,128]{2,1,0:T(8,128)S(1)} %get-tuple-element.8.s_in), custom_call_target="tpu_custom_call" | custom-call | tf_op jit(solution)/shard_map/factor/pallas_call | solution.py:501

commit v6 on v5

--- a/solution.py
+++ b/solution.py
@@ -113,109 +113,27 @@
         return high, middle, (rest - middle.astype(F32)).astype(BF16)
 
     lane = lax.broadcasted_iota(jnp.int32, (XB, RZ), 1)
-    group = lane // 4
+    narrow = lax.broadcasted_iota(jnp.int32, (8, RZ), 1) // 4
     member = lane % 4
     low_half = member < 2
 
     def split_fields(row):
         cols = pl.ds(pl.multiple_of(row * RZ, RZ), RZ)
         places = [lax.rem(f * RY + row, 32) for f in range(3)]
-        for b in range(N // XB):
-            here = pl.ds(b * XB, XB)
+        for b in range(N // 8):
+            here = pl.ds(b * 8, 8)
             faces_here = []
             for f in range(3):
-                value = fld[f, row + 2, pl.ds(XC + b * XB, XB), :]
+                value = fld[f, row + 2, pl.ds(XC + b * 8, 8), :]
                 faces_here.append(pltpu.roll(value, lax.rem(4 * places[f] + 2, RZ), 1))
                 high, middle, low = three_way(value)
                 halves[f, here, cols] = high
-                halves[f, pl.ds(N + b * XB, XB), cols] = middle
+                halves[f, pl.ds(N + b * 8, 8), cols] = middle
                 if f < 2:
                     thirds[f, here, cols] = low
-            first = jnp.where(group == places[0], faces_here[0], packs[0, here, :])
-            packs[0, here, :] = jnp.where(group == places[1], faces_here[1], first)
-            packs[1, here, :] = jnp.where(group == places[2], faces_here[2], packs[1, here, :])
-
-    def split_face(i, carry):
-        split_fields(i + (RY - 4) * (i // 2))
-        return carry
-
-    def split_rest(row, carry):
-        load(row).wait()
-        split_fields(row)
-        return carry
-
-    lax.fori_loop(0, 4, split_face, 0)
-    lax.fori_loop(2, RY - 2, split_rest, 0)
-
-    for b in range(N // XB):
-        here = pl.ds(b * XB, XB)
-        lo, hi = packs[0, here, :], packs[1, here, :]
-        pack_r[here, :] = jnp.where(low_half, lo, pltpu.roll(hi, 2, 1))
-        pack_l[here, :] = jnp.where(low_half, pltpu.roll(lo, RZ - 2, 1), hi)
-    z_halo = [
-        remote(pack_r, from_left, halo_send.at[4], halo_recv.at[4], right),
-        remote(pack_l, from_right, halo_send.at[5], halo_recv.at[5], left),
-    ]
-    for cp in z_halo:
-        cp.start()
-    sends += z_halo
-
-    eye = lax.broadcasted_iota(jnp.int32, (N, N), 0) == lax.broadcasted_iota(jnp.int32, (N, N), 1)
-    below = lax.broadcasted_iota(jnp.int32, (N, N), 0) > lax.broadcasted_iota(jnp.int32, (N, N), 1)
-
-    def gram(q, cols):
-        both = halves[q, :, cols]
-        full = lax.dot_general(both, both, (((1,), (1,)), ((), ())), preferred_element_type=F32)
-        return full[:N, :N] + full[:N, N:] + full[N:, :N] + full[N:, N:]
-
-    def diagonal(m):
-        return jnp.sum(jnp.where(eye, m, 0.0), axis=0, keepdims=True)
-
-    def fill(piece, squares, diags):
-        tail = jnp.concatenate(diags, axis=0)
-        for o in range(owners):
-            for k, value in enumerate(squares):
-                piece[o, k * own_rows:(k + 1) * own_rows, :] = value[o * own_rows:(o + 1) * own_rows, :]
-            piece[o, len(squares) * own_rows:, :] = tail
-
-    class Channel:
-        def __init__(self, piece, recv_a, sum_a, recv_b, sum_b, recv_c, rs_s, rs_r, ey_s, ey_r, ez_s, ez_r):
-            self.piece, self.recv_a, self.sum_a = piece, recv_a, sum_a
-            self.recv_b, self.sum_b, self.recv_c = recv_b, sum_b, recv_c
-            self.rs = [remote(piece.at[o], recv_a.at[k], rs_s.at[k], rs_r.at[k], to) for k, o, to in rs_peers]
-            self.ey = [remote(sum_a, recv_b.at[k], ey_s.at[k], ey_r.at[k], to) for k, to in ey_peers]
-            self.ez = [remote(sum_b, recv_c.at[k], ez_s.at[k], ez_r.at[k], to) for k, to in ez_peers]
-
-        def start(self, copies):
-            for cp in copies:
-                cp.start()
-
-        def collect(self, copies, recv, own):
-            for cp in copies:
-                cp.wait_recv()
-            for k in range(recv.shape[0]):
-                own = own + recv[k]
-            return own
-
-        def scatter(self):
-            self.start(self.rs)
-
-        def along_y(self):
-            self.sum_a[...] = self.collect(self.rs, self.recv_a, self.piece[me])
-            self.start(self.ey)
-
-        def along_z(self):
-            self.sum_b[...] = self.collect(self.ey, self.recv_b, self.sum_a[...])
-            self.start(self.ez)
-
-        def total(self):
-            return self.collect(self.ez, self.recv_c, self.sum_b[...])
-
-    early, late = Channel(*channels[:12]), Channel(*channels[12:])
-    everything = pl.ds(0, RY * RZ)
-    gu, gv, gw = (gram(f, everything) for f in range(3))
-    fill(early.piece, [jnp.where(below, gu, gv), gw], [diagonal(m) for m in (gu, gv, gw)])
-    early.scatter()
+            first = jnp.where(narrow == places[0], faces_here[0], packs[0, here, :])
+            packs[0, here, :] = jnp.where(narrow == places[1], faces_here[1], first)
+            packs[1, here, :] = jnp.where(narrow == places[2], faces_here[2], packs[1, here, :])
 
     wide = 2 * RZ
     step = lax.broadcasted_iota(jnp.int32, (RZ, RZ), 1) - lax.broadcasted_iota(jnp.int32, (RZ, RZ), 0)
@@ -242,6 +160,92 @@
                 a, b, c2 = (out[(2 * k + f) * rows:(2 * k + f + 1) * rows, r * RZ:(r + 1) * RZ] for k in range(3))
                 dz_buf[f, 2 * pair + r, pl.ds(at, rows), :] = a + b + c2
 
+    def split_face(i, carry):
+        split_fields(i + (RY - 4) * (i // 2))
+        return carry
+
+    def split_rest(pair, carry):
+        for r in range(2):
+            load(2 * pair + r).wait()
+        for part in range(PARTS):
+            inner_z(pair - 1, part)
+        for r in range(2):
+            split_fields(2 * pair + r)
+        return carry
+
+    lax.fori_loop(0, 4, split_face, 0)
+    lax.fori_loop(1, RY // 2 - 1, split_rest, 0)
+
+    for b in range(N // XB):
+        here = pl.ds(b * XB, XB)
+        lo, hi = packs[0, here, :], packs[1, here, :]
+        pack_r[here, :] = jnp.where(low_half, lo, pltpu.roll(hi, 2, 1))
+        pack_l[here, :] = jnp.where(low_half, pltpu.roll(lo, RZ - 2, 1), hi)
+    z_halo = [
+        remote(pack_r, from_left, halo_send.at[4], halo_recv.at[4], right),
+        remote(pack_l, from_right, halo_send.at[5], halo_recv.at[5], left),
+    ]
+    for cp in z_halo:
+        cp.start()
+    sends += z_halo
+
+    eye = lax.broadcasted_iota(jnp.int32, (N, N), 0) == lax.broadcasted_iota(jnp.int32, (N, N), 1)
+    below = lax.broadcasted_iota(jnp.int32, (N, N), 0) > lax.broadcasted_iota(jnp.int32, (N, N), 1)
+
+    def gram(q, cols):
+        both = halves[q, :, cols]
+        full = lax.dot_general(both, both, (((1,), (1,)), ((), ())), preferred_element_type=F32)
+        return full[:N, :N] + full[:N, N:] + full[N:, :N] + full[N:, N:]
+
+    def diagonal(m):
+        return jnp.sum(jnp.where(eye, m, 0.0), axis=0, keepdims=True)
+
+    def fill(piece, squares, diags):
+        tail = jnp.concatenate(diags, axis=0)
+        for o in range(owners):
+            for k, value in enumerate(squares):
+                piece[o, k * own_rows:(k + 1) * own_rows, :] = value[o * own_rows:(o + 1) * own_rows, :]
+            piece[o, len(squares) * own_rows:, :] = tail
+
+    class Channel:
+        def __init__(self, piece, recv_a, sum_a, recv_b, sum_b, recv_c, rs_s, rs_r, ey_s, ey_r, ez_s, ez_r):
+            self.piece, self.recv_a, self.sum_a = piece, recv_a, sum_a
+            self.recv_b, self.sum_b, self.recv_c = recv_b, sum_b, recv_c
+            self.rs = [remote(piece.at[o], recv_a.at[k], rs_s.at[k], rs_r.at[k], to) for k, o, to in rs_peers]
+            self.ey = [remote(sum_a, recv_b.at[k], ey_s.at[k], ey_r.at[k], to) for k, to in ey_peers]
+            self.ez = [remote(sum_b, recv_c.at[k], ez_s.at[k], ez_r.at[k], to) for k, to in ez_peers]
+
+        def start(self, copies):
+            for cp in copies:
+                cp.start()
+
+        def collect(self, copies, recv, own):
+            for cp in copies:
+                cp.wait_recv()
+            for k in range(recv.shape[0]):
+                own = own + recv[k]
+            return own
+
+        def scatter(self):
+            self.start(self.rs)
+
+        def along_y(self):
+            self.sum_a[...] = self.collect(self.rs, self.recv_a, self.piece[me])
+            self.start(self.ey)
+
+        def along_z(self):
+            self.sum_b[...] = self.collect(self.ey, self.recv_b, self.sum_a[...])
+            self.start(self.ez)
+
+        def total(self):
+            return self.collect(self.ez, self.recv_c, self.sum_b[...])
+
+    early, late = Channel(*channels[:12]), Channel(*channels[12:])
+    everything = pl.ds(0, RY * RZ)
+    gu, gv, gw = (gram(f, everything) for f in range(3))
+    fill(early.piece, [jnp.where(below, gu, gv), gw], [diagonal(m) for m in (gu, gv, gw)])
+    early.scatter()
+
     def derivative(m2, m1, p1, p2):
         return 8.0 * (p1 - m1) + (m2 - p2)
 
@@ -288,14 +292,15 @@
             enst[row, here, :] = e
             strn[row, here, :] = s
             for q, value in ((3, e), (4, s)):
-                high = value.astype(BF16)
-                halves[q, here, cols] = high
-                halves[q, pl.ds(N + b * XB, XB), cols] = (value - high.astype(F32)).astype(BF16)
+                for t in range(XB // 8):
+                    part = value[8 * t:8 * t + 8]
+                    high = part.astype(BF16)
+                    halves[q, pl.ds(b * XB + 8 * t, 8), cols] = high
+                    halves[q, pl.ds(N + b * XB + 8 * t, 8), cols] = (part - high.astype(F32)).astype(BF16)
 
     def inner_pair(pair, carry):
         each = N // XB // PARTS
         for part in range(PARTS):
-            inner_z(pair, part)
             for r in range(2):
                 blocks = range(part * each, (part + 1) * each)
                 wrapped_z(2 * pair + r, blocks)
@@ -303,11 +308,10 @@
         return carry
 
     def face_pair(i, carry):
-        pair = i * (RY // 2 - 1)
         for part in range(PARTS):
-            inner_z(pair, part)
+            inner_z(RY // 2 - 2 + i, part)
         for r in range(2):
-            wrapped_z(2 * pair + r, range(N // XB))
+            wrapped_z((RY - 2) * i + r, range(N // XB))
         return carry
 
     lax.fori_loop(1, RY // 2 - 1, inner_pair, 0)
@@ -390,8 +394,6 @@
         for q, (src, dst) in enumerate(((e_in, e_out), (s_in, s_out)))
         for r in range(RY)
     ]
-    for cp in stores:
-        cp.start()
     lane = lax.broadcasted_iota(jnp.int32, (8, N), 1)
     sub = lax.broadcasted_iota(jnp.int32, (8, N), 0)
     count = N // 8
@@ -408,6 +410,8 @@
             for i in range(p + 1, count)
             for k in range(8)
         }
+        for cp in stores[4 * p:4 * p + 4]:
+            cp.start()
         inverse, u, panel = [], {}, None
         for k in range(8):
             inverse.append(lax.rsqrt(s[k, k]))

time: 49.8 us -> 50.1 us (level)
  no operation moved by 1% of the time
where the time goes in v6:
time: 50.1 us; the launch traced here: 49.9 us
  Pallas kernels  49.3 us (98%)
  between operations  0.64 us (1%)
    pallas_call x1, Pallas kernels, per_device(): pl.pallas_call(body, out_shape=(grid_rows, grid_rows, jax.ShapeDtypeStruc...  44.2 us
    pallas_call x1, Pallas kernels, per_device(): pl.pallas_call(factor_kernel, out_shape=(whole, whole, jax.ShapeDtypeStru...  5.04 us

profile of v6, /device:TPU:1, one launch (start us, length us, event | category | flops | bytes accessed | tf_op | source)
XLA Modules:
  0.0 49.9 jit_solution(15533759829954789011)
XLA Ops:
  0.6 44.2 %stencil_gram.1 = (f32[16,128,128]{2,1,0:T(8,128)S(1)}, f32[16,128,128]{2,1,0:T(8,128)S(1)}, f32[128,128]{1,0:T(8,128)S(1)}) custom-call(f32[3,132,16,128]{3,2,1,0:T(8,128)} %refs_0_.1), custom_call_target="tpu_custom_call" | custom-call | tf_op jit(solution)/shard_map/stencil_gram/pallas_call | solution.py:473
  44.9 5.0 %factor.1 = (f32[128,16,128]{2,1,0:T(8,128)}, f32[128,16,128]{2,1,0:T(8,128)}, f32[128,128]{1,0:T(8,128)}) custom-call(f32[128,128]{1,0:T(8,128)S(1)} %get-tuple-element.6.cross, f32[16,128,128]{2,1,0:T(8,128)S(1)} %get-tuple-element.7.e_in, f32[16,128,128]{2,1,0:T(8,128)S(1)} %get-tuple-element.8.s_in), custom_call_target="tpu_custom_call" | custom-call | tf_op jit(solution)/shard_map/factor/pallas_call | solution.py:505

commit v7 on v5

--- a/solution.py
+++ b/solution.py
@@ -113,27 +113,27 @@
         return high, middle, (rest - middle.astype(F32)).astype(BF16)
 
     lane = lax.broadcasted_iota(jnp.int32, (XB, RZ), 1)
-    group = lane // 4
+    narrow = lax.broadcasted_iota(jnp.int32, (8, RZ), 1) // 4
     member = lane % 4
     low_half = member < 2
 
     def split_fields(row):
         cols = pl.ds(pl.multiple_of(row * RZ, RZ), RZ)
         places = [lax.rem(f * RY + row, 32) for f in range(3)]
-        for b in range(N // XB):
-            here = pl.ds(b * XB, XB)
+        for b in range(N // 8):
+            here = pl.ds(b * 8, 8)
             faces_here = []
             for f in range(3):
-                value = fld[f, row + 2, pl.ds(XC + b * XB, XB), :]
+                value = fld[f, row + 2, pl.ds(XC + b * 8, 8), :]
                 faces_here.append(pltpu.roll(value, lax.rem(4 * places[f] + 2, RZ), 1))
                 high, middle, low = three_way(value)
                 halves[f, here, cols] = high
-                halves[f, pl.ds(N + b * XB, XB), cols] = middle
+                halves[f, pl.ds(N + b * 8, 8), cols] = middle
                 if f < 2:
                     thirds[f, here, cols] = low
-            first = jnp.where(group == places[0], faces_here[0], packs[0, here, :])
-            packs[0, here, :] = jnp.where(group == places[1], faces_here[1], first)
-            packs[1, here, :] = jnp.where(group == places[2], faces_here[2], packs[1, here, :])
+            first = jnp.where(narrow == places[0], faces_here[0], packs[0, here, :])
+            packs[0, here, :] = jnp.where(narrow == places[1], faces_here[1], first)
+            packs[1, here, :] = jnp.where(narrow == places[2], faces_here[2], packs[1, here, :])
 
     def split_face(i, carry):
         split_fields(i + (RY - 4) * (i // 2))
@@ -288,9 +288,11 @@
             enst[row, here, :] = e
             strn[row, here, :] = s
             for q, value in ((3, e), (4, s)):
-                high = value.astype(BF16)
-                halves[q, here, cols] = high
-                halves[q, pl.ds(N + b * XB, XB), cols] = (value - high.astype(F32)).astype(BF16)
+                for t in range(XB // 8):
+                    part = value[8 * t:8 * t + 8]
+                    high = part.astype(BF16)
+                    halves[q, pl.ds(b * XB + 8 * t, 8), cols] = high
+                    halves[q, pl.ds(N + b * XB + 8 * t, 8), cols] = (part - high.astype(F32)).astype(BF16)
 
     def inner_pair(pair, carry):
         each = N // XB // PARTS
@@ -312,6 +314,15 @@
 
     lax.fori_loop(1, RY // 2 - 1, inner_pair, 0)
     lax.fori_loop(0, 2, face_pair, 0)
+    for way in range(2):
+        for r in range(2):
+            y_copy(way, r).wait_recv()
+
+    def face_row(i, carry):
+        without_z(i + (RY - 4) * (i // 2))
+        return carry
+
+    lax.fori_loop(0, 4, face_row, 0)
     for cp in z_halo:
         cp.wait_recv()
 
@@ -338,13 +349,9 @@
         return carry
 
     lax.fori_loop(1, RY // 2 - 1, inner_rows, 0)
-    for way in range(2):
-        for r in range(2):
-            y_copy(way, r).wait_recv()
     early.along_y()
     inside = [gram(3 + q, pl.ds(wide, (RY - 4) * RZ)) for q in range(2)]
     for row in faces:
-        without_z(row)
         with_z(row)
     ge, gs = (
         inside[q] + gram(3 + q, pl.ds(0, wide)) + gram(3 + q, pl.ds((RY - 2) * RZ, wide)) for q in range(2)
@@ -390,8 +397,6 @@
         for q, (src, dst) in enumerate(((e_in, e_out), (s_in, s_out)))
         for r in range(RY)
     ]
-    for cp in stores:
-        cp.start()
     lane = lax.broadcasted_iota(jnp.int32, (8, N), 1)
     sub = lax.broadcasted_iota(jnp.int32, (8, N), 0)
     count = N // 8
@@ -408,6 +413,8 @@
             for i in range(p + 1, count)
             for k in range(8)
         }
+        for cp in stores[4 * p:4 * p + 4]:
+            cp.start()
         inverse, u, panel = [], {}, None
         for k in range(8):
             inverse.append(lax.rsqrt(s[k, k]))

time: 49.8 us -> 49.8 us (level)
  no operation moved by 1% of the time
where the time goes in v7:
time: 49.8 us; the launch traced here: 49.7 us
  Pallas kernels  49 us (98%)
  between operations  0.64 us (1%)
    pallas_call x1, Pallas kernels, per_device(): pl.pallas_call(body, out_shape=(grid_rows, grid_rows, jax.ShapeDtypeStruc...  44 us
    pallas_call x1, Pallas kernels, per_device(): pl.pallas_call(factor_kernel, out_shape=(whole, whole, jax.ShapeDtypeStru...  5.04 us

profile of v7, /device:TPU:1, one launch (start us, length us, event | category | flops | bytes accessed | tf_op | source)
XLA Modules:
  0.0 49.7 jit_solution(17926256850796678665)
XLA Ops:
  0.6 44.0 %stencil_gram.1 = (f32[16,128,128]{2,1,0:T(8,128)S(1)}, f32[16,128,128]{2,1,0:T(8,128)S(1)}, f32[128,128]{1,0:T(8,128)S(1)}) custom-call(f32[3,132,16,128]{3,2,1,0:T(8,128)} %refs_0_.1), custom_call_target="tpu_custom_call" | custom-call | tf_op jit(solution)/shard_map/stencil_gram/pallas_call | solution.py:476
  44.6 5.0 %factor.1 = (f32[128,16,128]{2,1,0:T(8,128)}, f32[128,16,128]{2,1,0:T(8,128)}, f32[128,128]{1,0:T(8,128)}) custom-call(f32[128,128]{1,0:T(8,128)S(1)} %get-tuple-element.6.cross, f32[16,128,128]{2,1,0:T(8,128)S(1)} %get-tuple-element.7.e_in, f32[16,128,128]{2,1,0:T(8,128)S(1)} %get-tuple-element.8.s_in), custom_call_target="tpu_custom_call" | custom-call | tf_op jit(solution)/shard_map/factor/pallas_call | solution.py:508
